TPU v7x, 128 devices: a whole 4x4x4 slice. The times are simulated.
128 devices in a mesh: gx: 8 (over y_lo, z), gy: 16 (over y_hi, x, core).
Axes of the slice: x: 4, y: 4 (y_hi: 2, y_lo: 2; y = y_hi * 2 + y_lo), z: 4, core: 2. Of those that a mesh axis runs over, the one named last changes fastest.
Arguments:
- thickness: float32 [4096, 2048], P('gy', 'gx'), may hold values from 0.5 to 2
- driving: float32 [2, 4096, 2048], P(None, 'gy', 'gx'), may hold values from -6 to 6
- observed: float32 [2, 4096, 2048], P(None, 'gy', 'gx'), may hold values from -2 to 2
- control: float32 [64, 4096], P('gy'), may hold values from 0.5 to 1.5
- ice_mask: int32 [16, 8], replicated, may hold values 0 or 1
- tile_block: int32 [16, 8, 1], replicated, may hold values from 0 to 63
Outputs:
- vel_u: float32 [4096, 2048], P('gy', 'gx')
- vel_v: float32 [4096, 2048], P('gy', 'gx')
- grad_control: float32 [64, 4096], P('gy')
Inputs may be any that keep to these rules, and one draw needn't show every extreme that they name: `tile_block`: every one of the 64 control blocks is named by at least one tile.
All inputs are finite; a program needn't handle non-finite values.
Results may differ from a plain program's by a relative error of at most 0.00015.
Values sent between devices are 32-bit elements; how exact they have to be, the bound alone decides.
A program may use at most 64 MiB of HBM per device.

v0:
```python
import jax
import jax.numpy as jnp
from jax import lax
from jax.sharding import PartitionSpec as P

TILE = 256
CPC = 4
PIC = 4
SW = 2
ADJ = 6
CT = 64
COARSE = 4096


visc_scale = 0.1
strain_floor = 0.05


def with_halo(cells, sides, width):
    for axis, dim in sides:
        count = lax.axis_size(axis)
        ends = count - 1
        head = lax.slice_in_dim(cells, 0, width, axis=dim)
        tail = lax.slice_in_dim(cells, cells.shape[dim] - width, cells.shape[dim], axis=dim)
        cells = jnp.concatenate(
            [
                lax.ppermute(tail, axis, [(i, (i + 1) % count) for i in range(ends)]),
                cells,
                lax.ppermute(head, axis, [((i + 1) % count, i) for i in range(ends)]),
            ],
            axis=dim,
        )
    return cells


def viscosity(vel_pad, thick):
    speed_x = vel_pad[0]
    speed_y = vel_pad[1]
    dudx = 0.5 * (speed_x[1:-1, 2:] - speed_x[1:-1, :-2])
    dudy = 0.5 * (speed_x[2:, 1:-1] - speed_x[:-2, 1:-1])
    dvdx = 0.5 * (speed_y[1:-1, 2:] - speed_y[1:-1, :-2])
    dvdy = 0.5 * (speed_y[2:, 1:-1] - speed_y[:-2, 1:-1])
    shear = dudy + dvdx
    strain = dudx * dudx + dvdy * dvdy + dudx * dvdy + 0.25 * shear * shear + strain_floor
    return visc_scale * thick * jnp.power(strain, -1.0 / 3.0)


def coefficients(visc_pad, friction):
    center = visc_pad[1:-1, 1:-1]
    east_w = 0.5 * (center + visc_pad[1:-1, 2:])
    west_w = 0.5 * (center + visc_pad[1:-1, :-2])
    south_w = 0.5 * (center + visc_pad[2:, 1:-1])
    north_w = 0.5 * (center + visc_pad[:-2, 1:-1])
    diag_u = friction + 4.0 * (east_w + west_w) + south_w + north_w
    diag_v = friction + east_w + west_w + 4.0 * (south_w + north_w)
    return (visc_pad, east_w, west_w, south_w, north_w, diag_u, diag_v)


def relaxation(vel_pad, stencil_coef, forcing, ice_cells):
    visc_pad, east_w, west_w, south_w, north_w, diag_u, diag_v = stencil_coef
    speed_x = vel_pad[0]
    speed_y = vel_pad[1]
    flux_p = 2.0 * visc_pad[1:-1, :] * (0.5 * (speed_y[2:, :] - speed_y[:-2, :]))
    flux_q = visc_pad[:, 1:-1] * (0.5 * (speed_y[:, 2:] - speed_y[:, :-2]))
    cross_u = 0.5 * (flux_p[:, 2:] - flux_p[:, :-2]) + 0.5 * (flux_q[2:, :] - flux_q[:-2, :])
    flux_r = 2.0 * visc_pad[:, 1:-1] * (0.5 * (speed_x[:, 2:] - speed_x[:, :-2]))
    flux_s = visc_pad[1:-1, :] * (0.5 * (speed_x[2:, :] - speed_x[:-2, :]))
    cross_v = 0.5 * (flux_r[2:, :] - flux_r[:-2, :]) + 0.5 * (flux_s[:, 2:] - flux_s[:, :-2])
    near_u = (
        4.0 * (east_w * speed_x[1:-1, 2:] + west_w * speed_x[1:-1, :-2])
        + south_w * speed_x[2:, 1:-1]
        + north_w * speed_x[:-2, 1:-1]
    )
    near_v = (
        east_w * speed_y[1:-1, 2:]
        + west_w * speed_y[1:-1, :-2]
        + 4.0 * (south_w * speed_y[2:, 1:-1] + north_w * speed_y[:-2, 1:-1])
    )
    new_u = ice_cells * (forcing[0] + near_u + cross_u) / diag_u
    new_v = ice_cells * (forcing[1] + near_v + cross_v) / diag_v
    return jnp.stack([new_u, new_v])


def halo_velocity(field):
    return with_halo(field, (("gx", 2), ("gy", 1)), 1)


def per_device(thickness, driving, observed, control, ice_mask, tile_block):
    row_count, col_count = thickness.shape
    tile_count = col_count // TILE
    owned_rows = control.shape[0]
    row_tile = lax.axis_index("gy")
    col_tile = lax.axis_index("gx") * tile_count
    blocks = lax.dynamic_slice(tile_block[:, :, 0], (row_tile, col_tile), (1, tile_count))[0]
    ice_tiles = lax.dynamic_slice(ice_mask, (row_tile, col_tile), (1, tile_count))[0].astype(
        jnp.float32
    )
    ice_cells = jnp.broadcast_to(ice_tiles[None, :, None], (TILE, tile_count, TILE)).reshape(
        row_count, col_count
    )
    rates = jnp.exp(control)
    shard_rows = lax.all_gather(rates, "gy", axis=0, tiled=True)
    labels = jnp.arange(shard_rows.shape[0], dtype=jnp.int32)
    onehot = (blocks[:, None] == labels[None, :]).astype(jnp.float32)
    picked = jnp.dot(onehot, shard_rows, precision=lax.Precision.HIGHEST)
    friction = jnp.broadcast_to(
        picked.reshape(tile_count, CT, 1, CT, 1), (tile_count, CT, CPC, CT, CPC)
    )
    friction = (
        friction.reshape(tile_count, TILE, TILE).transpose(1, 0, 2).reshape(row_count, col_count)
    )
    velocity = jnp.zeros((2, row_count, col_count), jnp.float32)
    stencil_coef = None
    for picard in range(PIC):
        vel_pad = halo_velocity(velocity)
        visc_cells = viscosity(vel_pad, thickness)
        visc_pad = with_halo(visc_cells, (("gx", 1), ("gy", 0)), 1)
        stencil_coef = coefficients(visc_pad, friction)
        for sweep in range(SW):
            if sweep > 0:
                vel_pad = halo_velocity(velocity)
            velocity = relaxation(vel_pad, stencil_coef, driving, ice_cells)
    misfit = ice_cells * (velocity - observed)
    adjoint = jnp.zeros((2, row_count, col_count), jnp.float32)
    for sweep in range(ADJ):
        adjoint = relaxation(halo_velocity(adjoint), stencil_coef, misfit, ice_cells)
    cell_grad = -friction * (velocity[0] * adjoint[0] + velocity[1] * adjoint[1])
    tile_grad = cell_grad.reshape(CT, CPC, tile_count, CT, CPC).sum(axis=(1, 4))
    tile_grad = tile_grad.transpose(1, 0, 2).reshape(tile_count, COARSE)
    labels = jnp.arange(owned_rows * lax.axis_size("gy"), dtype=jnp.int32)
    onehot = (labels[:, None] == blocks[None, :]).astype(jnp.float32)
    partial_sum = lax.psum_scatter(
        jnp.dot(onehot, tile_grad, precision=lax.Precision.HIGHEST),
        "gy",
        scatter_dimension=0,
        tiled=True,
    )
    gradient = lax.psum(partial_sum, "gx")
    return (velocity[0], velocity[1], gradient)


def solution(mesh):
    return jax.shard_map(
        per_device,
        mesh=mesh,
        in_specs=(P("gy", "gx"), P(None, "gy", "gx"), P(None, "gy", "gx"), P("gy", None), P(), P()),
        out_specs=(P("gy", "gx"), P("gy", "gx"), P("gy", None)),
        check_vma=False,
    )
```

profile of v0, /device:TPU:0, one launch (start us, length us, event | category | flops | bytes accessed | tf_op | source)
XLA Modules:
  0.0 709.3 jit_solution(17794844136733789249)
XLA Ops:
  44.4 19.9 %all-gather.3.cloned.1.call-done = f32[16,4,4096]{2,1,0:T(4,128)} async-done(((f32[1,4,4096]{2,1,0:T(4,128)}), f32[16,4,4096]{2,1,0:T(4,128)}) %all-gather.3.cloned.1.call-update) | async-done | bytes 1048592 | tf_op jit(solution)/shard_map/all_gather | solution.py:102
  78.0 8.4 %broadcast_in_dim.8 = f32[256,256]{1,0:T(8,128)S(1)} reshape(f32[64,4,64,4]{3,2,1,0:T(8,128)} %broadcast_in_dim.7) | data formatting | bytes 524288 | tf_op jit(solution)/shard_map/broadcast_in_dim | solution.py:106
  110.1 5.2 collective-permute-start.12
  167.4 6.2 collective-permute-start.24
  187.6 7.1 %collective-permute-start.29 = (f32[256,1]{1,0:T(8,128)S(1)}, f32[256,1]{1,0:T(8,128)S(1)}, u32[]{:S(2)}, u32[]{:S(2)}) collective-permute-start(f32[256,1]{1,0:T(8,128)S(1)} %get-tuple-element.142), channel_id=1, source_target_pairs={{0,16},{16,32},{32,48},{48,64},{64,80},{80,96},{96,112},{1,17},{17... | collective-permute-start | bytes 3080 | tf_op jit(solution)/shard_map/ppermute | solution.py:27
  206.9 7.1 %collective-permute-start.32 = (f32[2,256,1]{2,1,0:T(8,128)S(1)}, f32[2,256,1]{2,1,0:T(8,128)S(1)}, u32[]{:S(2)}, u32[]{:S(2)}) collective-permute-start(f32[2,256,1]{2,1,0:T(8,128)S(1)} %get-tuple-element.99), channel_id=1, source_target_pairs={{0,16},{16,32},{32,48},{48,64},{64,80},{80,96},{96,112},{1,17},{17... | collective-permute-start | bytes 6152 | tf_op jit(solution)/shard_map/ppermute | solution.py:27
  229.5 7.1 %collective-permute-start.36 = (f32[2,256,1]{2,1,0:T(8,128)S(1)}, f32[2,256,1]{2,1,0:T(8,128)S(1)}, u32[]{:S(2)}, u32[]{:S(2)}) collective-permute-start(f32[2,256,1]{2,1,0:T(8,128)S(1)} %get-tuple-element.97), channel_id=1, source_target_pairs={{0,16},{16,32},{32,48},{48,64},{64,80},{80,96},{96,112},{1,17},{17... | collective-permute-start | bytes 6152 | tf_op jit(solution)/shard_map/ppermute | solution.py:27
  241.9 5.5 collective-permute-start.38
  250.6 7.1 %collective-permute-start.41 = (f32[256,1]{1,0:T(8,128)S(1)}, f32[256,1]{1,0:T(8,128)S(1)}, u32[]{:S(2)}, u32[]{:S(2)}) collective-permute-start(f32[256,1]{1,0:T(8,128)S(1)} %get-tuple-element.140), channel_id=1, source_target_pairs={{0,16},{16,32},{32,48},{48,64},{64,80},{80,96},{96,112},{1,17},{17... | collective-permute-start | bytes 3080 | tf_op jit(solution)/shard_map/ppermute | solution.py:27
  262.1 5.2 collective-permute-start.43
  271.0 7.1 %collective-permute-start.44 = (f32[2,256,1]{2,1,0:T(8,128)S(1)}, f32[2,256,1]{2,1,0:T(8,128)S(1)}, u32[]{:S(2)}, u32[]{:S(2)}) collective-permute-start(f32[2,256,1]{2,1,0:T(8,128)S(1)} %get-tuple-element.95), channel_id=1, source_target_pairs={{0,16},{16,32},{32,48},{48,64},{64,80},{80,96},{96,112},{1,17},{17... | collective-permute-start | bytes 6152 | tf_op jit(solution)/shard_map/ppermute | solution.py:27
  284.1 5.2 collective-permute-start.46
  295.4 7.1 %collective-permute-start.48 = (f32[2,256,1]{2,1,0:T(8,128)S(1)}, f32[2,256,1]{2,1,0:T(8,128)S(1)}, u32[]{:S(2)}, u32[]{:S(2)}) collective-permute-start(f32[2,256,1]{2,1,0:T(8,128)S(1)} %get-tuple-element.93), channel_id=1, source_target_pairs={{0,16},{16,32},{32,48},{48,64},{64,80},{80,96},{96,112},{1,17},{17... | collective-permute-start | bytes 6152 | tf_op jit(solution)/shard_map/ppermute | solution.py:27
  317.9 7.1 %collective-permute-start.52 = (f32[2,256,1]{2,1,0:T(8,128)S(1)}, f32[2,256,1]{2,1,0:T(8,128)S(1)}, u32[]{:S(2)}, u32[]{:S(2)}) collective-permute-start(f32[2,256,1]{2,1,0:T(8,128)S(1)} %get-tuple-element.91), channel_id=1, source_target_pairs={{0,16},{16,32},{32,48},{48,64},{64,80},{80,96},{96,112},{1,17},{17... | collective-permute-start | bytes 6152 | tf_op jit(solution)/shard_map/ppermute | solution.py:27
  340.3 6.8 collective-permute-start.56
  352.3 6.1 collective-permute-start.58
  363.0 7.1 %collective-permute-start.60 = (f32[2,256,1]{2,1,0:T(8,128)S(1)}, f32[2,256,1]{2,1,0:T(8,128)S(1)}, u32[]{:S(2)}, u32[]{:S(2)}) collective-permute-start(f32[2,256,1]{2,1,0:T(8,128)S(1)} %get-tuple-element.87), channel_id=1, source_target_pairs={{0,16},{16,32},{32,48},{48,64},{64,80},{80,96},{96,112},{1,17},{17... | collective-permute-start | bytes 6152 | tf_op jit(solution)/shard_map/ppermute | solution.py:27
  375.4 8.5 %collective-permute-start.62 = (f32[2,1,258]{2,1,0:T(1,128)S(1)}, f32[2,1,258]{2,1,0:T(1,128)S(1)}, u32[]{:S(2)}, u32[]{:S(2)}) collective-permute-start(f32[2,1,258]{2,1,0:T(1,128)S(1)} %get-tuple-element.36), channel_id=1, source_target_pairs={{0,1},{1,2},{2,3},{3,4},{4,5},{5,6},{6,7},{7,8},{8,9},{9,10},{10,1... | collective-permute-start | bytes 6200 | tf_op jit(solution)/shard_map/ppermute | solution.py:27
  388.3 7.1 %collective-permute-start.64 = (f32[2,256,1]{2,1,0:T(8,128)S(1)}, f32[2,256,1]{2,1,0:T(8,128)S(1)}, u32[]{:S(2)}, u32[]{:S(2)}) collective-permute-start(f32[2,256,1]{2,1,0:T(8,128)S(1)} %get-tuple-element.85), channel_id=1, source_target_pairs={{0,16},{16,32},{32,48},{48,64},{64,80},{80,96},{96,112},{1,17},{17... | collective-permute-start | bytes 6152 | tf_op jit(solution)/shard_map/ppermute | solution.py:27
  399.4 7.7 %collective-permute-start.66 = (f32[2,1,258]{2,1,0:T(1,128)S(1)}, f32[2,1,258]{2,1,0:T(1,128)S(1)}, u32[]{:S(2)}, u32[]{:S(2)}) collective-permute-start(f32[2,1,258]{2,1,0:T(1,128)S(1)} %get-tuple-element.34), channel_id=1, source_target_pairs={{0,1},{1,2},{2,3},{3,4},{4,5},{5,6},{6,7},{7,8},{8,9},{9,10},{10,1... | collective-permute-start | bytes 6200 | tf_op jit(solution)/shard_map/ppermute | solution.py:27
  409.0 7.8 %collective-permute-done.67 = f32[2,1,258]{2,1,0:T(1,128)S(1)} collective-permute-done((f32[2,1,258]{2,1,0:T(1,128)S(1)}, f32[2,1,258]{2,1,0:T(1,128)S(1)}, u32[]{:S(2)}, u32[]{:S(2)}) %collective-permute-start.67) | collective-permute-done | bytes 2096 | tf_op jit(solution)/shard_map/ppermute | solution.py:29
  419.0 10.1 %reshape.213 = f32[64,4,64,4]{3,2,1,0:T(8,128)} reshape(f32[256,256]{1,0:T(8,128)S(1)} %fusion.161) | data formatting | bytes 524288 | tf_op jit(solution)/shard_map/reshape | solution.py:128
  435.7 188.1 %all-reduce.6.cloned.1.call-done = f32[64,4096]{1,0:T(8,128)} async-done(((f32[64,4096]{1,0:T(8,128)}), f32[64,4096]{1,0:T(8,128)}) %all-reduce.6.cloned.1.call-update) | async-done | bytes 1048592
  625.4 75.7 %all-reduce.4.cloned.1.call-done = f32[4,4096]{1,0:T(4,128)} async-done(((f32[4,4096]{1,0:T(4,128)}), f32[4,4096]{1,0:T(4,128)}) %all-reduce.4.cloned.1.call-update) | async-done | bytes 65552 | tf_op jit(solution)/shard_map/psum | solution.py:138
  (304 shorter events, 261.9 us)
Async XLA Ops:
  7.2 57.2 %all-gather.3.cloned.1.call-start = ((), (), s32[]{:S(2)}) async-start(), calls=%async_computation.1 | async-start | bytes 1114112 | tf_op jit(solution)/shard_map/all_gather | solution.py:102
  14.6 609.2 %all-reduce.6.cloned.1.call-start = ((), (), s32[]{:S(2)}) async-start(), calls=%async_computation.2 | async-start | bytes 2097152
  108.8 11.4 %collective-permute-start.13 = (f32[2,256,1]{2,1,0:T(8,128)S(1)}, f32[2,256,1]{2,1,0:T(8,128)S(1)}, u32[]{:S(2)}, u32[]{:S(2)}) collective-permute-start(f32[2,256,1]{2,1,0:T(8,128)S(1)} %get-tuple-element.106), channel_id=1, source_target_pairs={{16,0},{32,16},{48,32},{64,48},{80,64},{96,80},{112,96},{17,1},{33... | collective-permute-start | bytes 6152 | tf_op jit(solution)/shard_map/ppermute | solution.py:29
  110.1 11.7 %collective-permute-start.12 = (f32[2,256,1]{2,1,0:T(8,128)S(1)}, f32[2,256,1]{2,1,0:T(8,128)S(1)}, u32[]{:S(2)}, u32[]{:S(2)}) collective-permute-start(f32[2,256,1]{2,1,0:T(8,128)S(1)} %get-tuple-element.105), channel_id=1, source_target_pairs={{0,16},{16,32},{32,48},{48,64},{64,80},{80,96},{96,112},{1,17},{17... | collective-permute-start | bytes 6152 | tf_op jit(solution)/shard_map/ppermute | solution.py:27
  145.6 10.7 %collective-permute-start.21 = (f32[2,256,1]{2,1,0:T(8,128)S(1)}, f32[2,256,1]{2,1,0:T(8,128)S(1)}, u32[]{:S(2)}, u32[]{:S(2)}) collective-permute-start(f32[2,256,1]{2,1,0:T(8,128)S(1)} %get-tuple-element.104), channel_id=1, source_target_pairs={{16,0},{32,16},{48,32},{64,48},{80,64},{96,80},{112,96},{17,1},{33... | collective-permute-start | bytes 6152 | tf_op jit(solution)/shard_map/ppermute | solution.py:29
  146.9 11.2 %collective-permute-start.20 = (f32[2,256,1]{2,1,0:T(8,128)S(1)}, f32[2,256,1]{2,1,0:T(8,128)S(1)}, u32[]{:S(2)}, u32[]{:S(2)}) collective-permute-start(f32[2,256,1]{2,1,0:T(8,128)S(1)} %get-tuple-element.103), channel_id=1, source_target_pairs={{0,16},{16,32},{32,48},{48,64},{64,80},{80,96},{96,112},{1,17},{17... | collective-permute-start | bytes 6152 | tf_op jit(solution)/shard_map/ppermute | solution.py:27
  166.1 11.6 %collective-permute-start.25 = (f32[2,256,1]{2,1,0:T(8,128)S(1)}, f32[2,256,1]{2,1,0:T(8,128)S(1)}, u32[]{:S(2)}, u32[]{:S(2)}) collective-permute-start(f32[2,256,1]{2,1,0:T(8,128)S(1)} %get-tuple-element.102), channel_id=1, source_target_pairs={{16,0},{32,16},{48,32},{64,48},{80,64},{96,80},{112,96},{17,1},{33... | collective-permute-start | bytes 6152 | tf_op jit(solution)/shard_map/ppermute | solution.py:29
  167.4 12.1 %collective-permute-start.24 = (f32[2,256,1]{2,1,0:T(8,128)S(1)}, f32[2,256,1]{2,1,0:T(8,128)S(1)}, u32[]{:S(2)}, u32[]{:S(2)}) collective-permute-start(f32[2,256,1]{2,1,0:T(8,128)S(1)} %get-tuple-element.101), channel_id=1, source_target_pairs={{0,16},{16,32},{32,48},{48,64},{64,80},{80,96},{96,112},{1,17},{17... | collective-permute-start | bytes 6152 | tf_op jit(solution)/shard_map/ppermute | solution.py:27
  205.6 11.2 %collective-permute-start.33 = (f32[2,256,1]{2,1,0:T(8,128)S(1)}, f32[2,256,1]{2,1,0:T(8,128)S(1)}, u32[]{:S(2)}, u32[]{:S(2)}) collective-permute-start(f32[2,256,1]{2,1,0:T(8,128)S(1)} %get-tuple-element.100), channel_id=1, source_target_pairs={{16,0},{32,16},{48,32},{64,48},{80,64},{96,80},{112,96},{17,1},{33... | collective-permute-start | bytes 6152 | tf_op jit(solution)/shard_map/ppermute | solution.py:29
  206.9 11.6 %collective-permute-start.32 = (f32[2,256,1]{2,1,0:T(8,128)S(1)}, f32[2,256,1]{2,1,0:T(8,128)S(1)}, u32[]{:S(2)}, u32[]{:S(2)}) collective-permute-start(f32[2,256,1]{2,1,0:T(8,128)S(1)} %get-tuple-element.99), channel_id=1, source_target_pairs={{0,16},{16,32},{32,48},{48,64},{64,80},{80,96},{96,112},{1,17},{17... | collective-permute-start | bytes 6152 | tf_op jit(solution)/shard_map/ppermute | solution.py:27
  228.2 10.8 %collective-permute-start.37 = (f32[2,256,1]{2,1,0:T(8,128)S(1)}, f32[2,256,1]{2,1,0:T(8,128)S(1)}, u32[]{:S(2)}, u32[]{:S(2)}) collective-permute-start(f32[2,256,1]{2,1,0:T(8,128)S(1)} %get-tuple-element.98), channel_id=1, source_target_pairs={{16,0},{32,16},{48,32},{64,48},{80,64},{96,80},{112,96},{17,1},{33... | collective-permute-start | bytes 6152 | tf_op jit(solution)/shard_map/ppermute | solution.py:29
  229.5 11.0 %collective-permute-start.36 = (f32[2,256,1]{2,1,0:T(8,128)S(1)}, f32[2,256,1]{2,1,0:T(8,128)S(1)}, u32[]{:S(2)}, u32[]{:S(2)}) collective-permute-start(f32[2,256,1]{2,1,0:T(8,128)S(1)} %get-tuple-element.97), channel_id=1, source_target_pairs={{0,16},{16,32},{32,48},{48,64},{64,80},{80,96},{96,112},{1,17},{17... | collective-permute-start | bytes 6152 | tf_op jit(solution)/shard_map/ppermute | solution.py:27
  269.7 11.2 %collective-permute-start.45 = (f32[2,256,1]{2,1,0:T(8,128)S(1)}, f32[2,256,1]{2,1,0:T(8,128)S(1)}, u32[]{:S(2)}, u32[]{:S(2)}) collective-permute-start(f32[2,256,1]{2,1,0:T(8,128)S(1)} %get-tuple-element.96), channel_id=1, source_target_pairs={{16,0},{32,16},{48,32},{64,48},{80,64},{96,80},{112,96},{17,1},{33... | collective-permute-start | bytes 6152 | tf_op jit(solution)/shard_map/ppermute | solution.py:29
  271.0 11.7 %collective-permute-start.44 = (f32[2,256,1]{2,1,0:T(8,128)S(1)}, f32[2,256,1]{2,1,0:T(8,128)S(1)}, u32[]{:S(2)}, u32[]{:S(2)}) collective-permute-start(f32[2,256,1]{2,1,0:T(8,128)S(1)} %get-tuple-element.95), channel_id=1, source_target_pairs={{0,16},{16,32},{32,48},{48,64},{64,80},{80,96},{96,112},{1,17},{17... | collective-permute-start | bytes 6152 | tf_op jit(solution)/shard_map/ppermute | solution.py:27
  294.1 11.3 %collective-permute-start.49 = (f32[2,256,1]{2,1,0:T(8,128)S(1)}, f32[2,256,1]{2,1,0:T(8,128)S(1)}, u32[]{:S(2)}, u32[]{:S(2)}) collective-permute-start(f32[2,256,1]{2,1,0:T(8,128)S(1)} %get-tuple-element.94), channel_id=1, source_target_pairs={{16,0},{32,16},{48,32},{64,48},{80,64},{96,80},{112,96},{17,1},{33... | collective-permute-start | bytes 6152 | tf_op jit(solution)/shard_map/ppermute | solution.py:29
  295.4 11.7 %collective-permute-start.48 = (f32[2,256,1]{2,1,0:T(8,128)S(1)}, f32[2,256,1]{2,1,0:T(8,128)S(1)}, u32[]{:S(2)}, u32[]{:S(2)}) collective-permute-start(f32[2,256,1]{2,1,0:T(8,128)S(1)} %get-tuple-element.93), channel_id=1, source_target_pairs={{0,16},{16,32},{32,48},{48,64},{64,80},{80,96},{96,112},{1,17},{17... | collective-permute-start | bytes 6152 | tf_op jit(solution)/shard_map/ppermute | solution.py:27
  316.6 11.7 %collective-permute-start.53 = (f32[2,256,1]{2,1,0:T(8,128)S(1)}, f32[2,256,1]{2,1,0:T(8,128)S(1)}, u32[]{:S(2)}, u32[]{:S(2)}) collective-permute-start(f32[2,256,1]{2,1,0:T(8,128)S(1)} %get-tuple-element.92), channel_id=1, source_target_pairs={{16,0},{32,16},{48,32},{64,48},{80,64},{96,80},{112,96},{17,1},{33... | collective-permute-start | bytes 6152 | tf_op jit(solution)/shard_map/ppermute | solution.py:29
  317.9 12.1 %collective-permute-start.52 = (f32[2,256,1]{2,1,0:T(8,128)S(1)}, f32[2,256,1]{2,1,0:T(8,128)S(1)}, u32[]{:S(2)}, u32[]{:S(2)}) collective-permute-start(f32[2,256,1]{2,1,0:T(8,128)S(1)} %get-tuple-element.91), channel_id=1, source_target_pairs={{0,16},{16,32},{32,48},{48,64},{64,80},{80,96},{96,112},{1,17},{17... | collective-permute-start | bytes 6152 | tf_op jit(solution)/shard_map/ppermute | solution.py:27
  340.3 10.7 %collective-permute-start.56 = (f32[2,256,1]{2,1,0:T(8,128)S(1)}, f32[2,256,1]{2,1,0:T(8,128)S(1)}, u32[]{:S(2)}, u32[]{:S(2)}) collective-permute-start(f32[2,256,1]{2,1,0:T(8,128)S(1)} %get-tuple-element.89), channel_id=1, source_target_pairs={{0,16},{16,32},{32,48},{48,64},{64,80},{80,96},{96,112},{1,17},{17... | collective-permute-start | bytes 6152 | tf_op jit(solution)/shard_map/ppermute | solution.py:27
  361.7 10.8 %collective-permute-start.61 = (f32[2,256,1]{2,1,0:T(8,128)S(1)}, f32[2,256,1]{2,1,0:T(8,128)S(1)}, u32[]{:S(2)}, u32[]{:S(2)}) collective-permute-start(f32[2,256,1]{2,1,0:T(8,128)S(1)} %get-tuple-element.88), channel_id=1, source_target_pairs={{16,0},{32,16},{48,32},{64,48},{80,64},{96,80},{112,96},{17,1},{33... | collective-permute-start | bytes 6152 | tf_op jit(solution)/shard_map/ppermute | solution.py:29
  363.0 11.0 %collective-permute-start.60 = (f32[2,256,1]{2,1,0:T(8,128)S(1)}, f32[2,256,1]{2,1,0:T(8,128)S(1)}, u32[]{:S(2)}, u32[]{:S(2)}) collective-permute-start(f32[2,256,1]{2,1,0:T(8,128)S(1)} %get-tuple-element.87), channel_id=1, source_target_pairs={{0,16},{16,32},{32,48},{48,64},{64,80},{80,96},{96,112},{1,17},{17... | collective-permute-start | bytes 6152 | tf_op jit(solution)/shard_map/ppermute | solution.py:27
  387.0 10.8 %collective-permute-start.65 = (f32[2,256,1]{2,1,0:T(8,128)S(1)}, f32[2,256,1]{2,1,0:T(8,128)S(1)}, u32[]{:S(2)}, u32[]{:S(2)}) collective-permute-start(f32[2,256,1]{2,1,0:T(8,128)S(1)} %get-tuple-element.86), channel_id=1, source_target_pairs={{16,0},{32,16},{48,32},{64,48},{80,64},{96,80},{112,96},{17,1},{33... | collective-permute-start | bytes 6152 | tf_op jit(solution)/shard_map/ppermute | solution.py:29
  388.3 11.0 %collective-permute-start.64 = (f32[2,256,1]{2,1,0:T(8,128)S(1)}, f32[2,256,1]{2,1,0:T(8,128)S(1)}, u32[]{:S(2)}, u32[]{:S(2)}) collective-permute-start(f32[2,256,1]{2,1,0:T(8,128)S(1)} %get-tuple-element.85), channel_id=1, source_target_pairs={{0,16},{16,32},{32,48},{48,64},{64,80},{80,96},{96,112},{1,17},{17... | collective-permute-start | bytes 6152 | tf_op jit(solution)/shard_map/ppermute | solution.py:27
  434.4 266.7 %all-reduce.4.cloned.1.call-start = ((), (), s32[]{:S(2)}) async-start(), calls=%async_computation | async-start | bytes 131072 | tf_op jit(solution)/shard_map/psum | solution.py:138
  (62 other events, 934.4 us)
Sparse Core Ops, SparseCore 0:
  14.8 49.5 all-gather.2
  434.5 189.2 all-reduce.5
  627.0 74.0 all-reduce.3
where the time goes:
time: 719 us; the launch traced here: 709 us
  waiting for transfers between devices  373 us (52%)
  starting transfers between devices  229 us (32%)
  other arithmetic  48.5 us (7%)
  local copies, waits for them, and re-layouts  37.6 us (5%)
  between operations  16.9 us (2%)
    unnamed x4, waiting for transfers between devices  188 us
    ppermute x34, starting transfers between devices, with_halo(): lax.ppermute(tail, axis, [(i, (i + 1) % count) for i in range(ends)])  185 us
    psum x1, waiting for transfers between devices, per_device(): gradient = lax.psum(partial_sum, 'gx')  75.7 us
    ppermute x34, waiting for transfers between devices, with_halo(): lax.ppermute(head, axis, [((i + 1) % count, i) for i in range(ends)])  53.8 us
    ppermute x34, starting transfers between devices, with_halo(): lax.ppermute(head, axis, [((i + 1) % count, i) for i in range(ends)])  43.9 us
    ppermute x34, waiting for transfers between devices, with_halo(): lax.ppermute(tail, axis, [(i, (i + 1) % count) for i in range(ends)])  35.8 us
    all_gather x1, waiting for transfers between devices, per_device(): shard_rows = lax.all_gather(rates, 'gy', axis=0, tiled=True)  19.9 us
    another operation x36, other arithmetic, relaxation(): return jnp.stack([new_u, new_v])  15.8 us
  transfers between devices with their start and end apart: 71, of which 52 were waited for; matrix products, arithmetic and copies ran while one was open for 2% of the time, Pallas kernels for 0%

commit v1 on v0

v1 whole, which is shorter than its diff:
```python
import functools

import jax
import jax.numpy as jnp
import numpy as np
from jax import lax
from jax.experimental import pallas as pl
from jax.experimental.pallas import tpu as pltpu
from jax.sharding import PartitionSpec as P

TILE = 256
HALO = 16
EXT = TILE + 2 * HALO
STRIP = EXT // 8
LT = 3
PIC = 4
ADJ = 6
GX = 8
GY = 16
UNROLL = 3
MESH = pl.DeviceIdType.MESH
F32 = jnp.float32

visc_scale = 0.1
strain_floor = 0.05


def exchange_kernel(
    blk, thick, drv, obs, ctl,
    h_north, h_south, h_west, h_east, coarse,
    pack_w, pack_e, c_send, c_recv,
    g_send, g_recv, x_send, x_recv, n_send, n_recv,
):
    gx = lax.axis_index("gx")
    gy = lax.axis_index("gy")

    def dev(dy, dx):
        return (lax.rem(gx + dx + GX, GX), lax.rem(gy + dy + GY, GY))

    barrier = pltpu.get_barrier_semaphore()
    peers = [(dy, 0) for dy in range(1, GY)] + [(dy, dx) for dx in (-1, 1) for dy in (-1, 0, 1)]
    for dy, dx in peers:
        pl.semaphore_signal(barrier, inc=1, device_id=dev(dy, dx), device_id_type=MESH)

    for off in range(GY):
        dest = lax.rem(gy + off, GY)
        c_send[off] = ctl[lax.rem(blk[dest, gx], 4)]
    c_recv[0] = c_send[0]

    lane = lax.broadcasted_iota(jnp.int32, (8, 128), 1)

    @pl.loop(0, TILE // 8)
    def _(t):
        rows = pl.ds(pl.multiple_of(t * 8, 8), 8)
        fields = [thick, drv.at[0], drv.at[1], obs.at[0], obs.at[1]]
        west = fields[0][rows, pl.ds(0, 128)]
        east = fields[0][rows, pl.ds(128, 128)]
        for f in range(1, 5):
            west = jnp.where(lane < 16 * f, west, pltpu.roll(fields[f][rows, pl.ds(0, 128)], 16 * f, 1))
            east = jnp.where(
                lane >= 128 - 16 * f, east, pltpu.roll(fields[f][rows, pl.ds(128, 128)], 128 - 16 * f, 1)
            )
        pack_w[rows, :] = west
        pack_e[rows, :] = east

    pl.semaphore_wait(barrier, len(peers))

    def remote(src, dst, ss, rs, to):
        return pltpu.make_async_remote_copy(
            src_ref=src, dst_ref=dst, send_sem=ss, recv_sem=rs, device_id=to, device_id_type=MESH
        )

    gathers = [
        remote(c_send.at[off], c_recv.at[off], g_send.at[off], g_recv.at[off], dev(off, 0))
        for off in range(1, GY)
    ]
    for g in gathers:
        g.start()

    lo, hi, full = pl.ds(0, HALO), pl.ds(TILE - HALO, HALO), pl.ds(0, TILE)
    moves = [
        (pack_e, h_west.at[pl.ds(HALO, TILE)], (0, 1)),
        (pack_w, h_east.at[pl.ds(HALO, TILE)], (0, -1)),
        (thick.at[hi], h_north.at[0], (1, 0)),
        (thick.at[lo], h_south.at[0], (-1, 0)),
        (drv.at[:, hi], h_north.at[pl.ds(1, 2)], (1, 0)),
        (drv.at[:, lo], h_south.at[pl.ds(1, 2)], (-1, 0)),
        (obs.at[:, hi], h_north.at[pl.ds(3, 2)], (1, 0)),
        (obs.at[:, lo], h_south.at[pl.ds(3, 2)], (-1, 0)),
        (pack_e.at[hi], h_west.at[pl.ds(0, HALO)], (1, 1)),
        (pack_e.at[lo], h_west.at[pl.ds(TILE + HALO, HALO)], (-1, 1)),
        (pack_w.at[hi], h_east.at[pl.ds(0, HALO)], (1, -1)),
        (pack_w.at[lo], h_east.at[pl.ds(TILE + HALO, HALO)], (-1, -1)),
    ]
    halos = [
        remote(src, dst, x_send.at[n], x_recv.at[n], dev(*to)) for n, (src, dst, to) in enumerate(moves)
    ]
    for h in halos:
        h.start()

    for g in gathers:
        g.wait_recv()
    mine = blk[gy, gx]
    coarse[4] = c_recv[lax.rem(gy - mine // 4 + GY, GY)]
    near = []
    for dy in (-1, 0, 1):
        for dx in (-1, 0, 1):
            if (dy, dx) != (0, 0):
                slot = (1 - dy) * 3 + (1 - dx)
                near.append(
                    remote(coarse.at[4], coarse.at[slot], n_send.at[slot], n_recv.at[slot], dev(dy, dx))
                )
    for n in near:
        n.start()
    for h in halos:
        h.wait()
    for n in near:
        n.wait()
    for g in gathers:
        g.wait_send()


def solve_kernel(
    ice_ref, thick, drv, obs, h_north, h_south, h_west, h_east, coarse,
    out_u, out_v, grad,
    nat, cext, T, FU, FV, OU, OV, FR, IC, H, A, B, IU, IV,
    U0, UE0, UW0, V0, VE0, VW0, U1, UE1, UW1, V1, VE1, VW1,
):
    gx = lax.axis_index("gx")
    gy = lax.axis_index("gy")
    lane = lax.broadcasted_iota(jnp.int32, (8, 128), 1)
    sub = lax.broadcasted_iota(jnp.int32, (8, 128), 0)
    lane3 = lax.broadcasted_iota(jnp.int32, (LT, 8, 128), 2)
    sides = ((-1, -1), (-1, 0), (-1, 1), (0, -1), (0, 0), (0, 1), (1, -1), (1, 0), (1, 1))
    inside, iced = {}, {}
    for dy, dx in sides:
        ok = (gy + dy >= 0) & (gy + dy < GY) & (gx + dx >= 0) & (gx + dx < GX)
        flag = ok.astype(F32)
        at = ice_ref[jnp.clip(gy + dy, 0, GY - 1), jnp.clip(gx + dx, 0, GX - 1)]
        inside[dy, dx] = flag
        iced[dy, dx] = flag * at.astype(F32)

    def region(i, table):
        row = sub * STRIP + i

        def by_row(dx):
            return jnp.where(
                row < HALO, table[-1, dx], jnp.where(row < HALO + TILE, table[0, dx], table[1, dx])
            )

        center = by_row(0)
        edge = jnp.where(lane < HALO, by_row(1), jnp.where(lane >= 128 - HALO, by_row(-1), 0.0))
        return jnp.stack([center, center, edge])

    def west(x):
        y = pltpu.roll(x, 1, 2)
        return jnp.where(lane3 == 0, jnp.concatenate([y[2:], y[:2]], axis=0), y)

    def east(x):
        y = pltpu.roll(x, 127, 2)
        return jnp.where(lane3 == 127, jnp.concatenate([y[1:], y[:1]], axis=0), y)

    def wrap(refs):
        for ref in refs:
            ref[0] = pltpu.roll(ref[STRIP], 1, 1)
            ref[STRIP + 1] = pltpu.roll(ref[1], 7, 1)

    fields = [(thick, T), (drv.at[0], FU), (drv.at[1], FV), (obs.at[0], OU), (obs.at[1], OV)]
    for f, (src, dst) in enumerate(fields):
        for c in range(2):
            cols = pl.ds(c * 128, 128)
            nat[c, pl.ds(0, HALO)] = h_north[f, :, cols]
            nat[c, pl.ds(HALO, TILE)] = src[:, cols]
            nat[c, pl.ds(HALO + TILE, HALO)] = h_south[f, :, cols]

        @pl.loop(0, EXT // 8)
        def _(t):
            rows = pl.ds(pl.multiple_of(t * 8, 8), 8)
            right = h_east[rows, :]
            left = h_west[rows, :]
            if f > 0:
                right = pltpu.roll(right, 128 - 16 * f, 1)
                left = pltpu.roll(left, 16 * f, 1)
            nat[2, rows] = jnp.where(lane < HALO, right, jnp.where(lane >= 128 - HALO, left, 0.0))

        @pl.loop(0, STRIP)
        def _(i):
            x = jnp.stack([nat[c, pl.ds(i, 8, stride=STRIP), :] for c in range(LT)])
            if f == 0:
                x = x * region(i, inside)
                IC[i] = region(i, iced)
            dst[i] = x

    cext[...] = jnp.zeros_like(cext)
    for g, dx in enumerate((0, 1, -1)):
        cext[g, pl.ds(0, 2)] = jnp.exp(coarse[0 * 3 + 1 + dx, pl.ds(30, 2), :])
        cext[g, pl.ds(2, 32)] = jnp.exp(coarse[1 * 3 + 1 + dx])
        cext[g, pl.ds(34, 2)] = jnp.exp(coarse[2 * 3 + 1 + dx, pl.ds(0, 2), :])

    def hot(rows, cols, fn):
        r = lax.broadcasted_iota(jnp.int32, (rows, cols), 0)
        c = lax.broadcasted_iota(jnp.int32, (rows, cols), 1)
        return jnp.where(fn(r, c), 1.0, 0.0).astype(F32)

    def mul(a, b):
        return jnp.dot(a, b, precision=lax.Precision.HIGHEST, preferred_element_type=F32)

    wide = []
    for par in range(2):
        spread_c = hot(128, TILE, lambda r, c: r == par * 64 + c // 4)
        spread_e = hot(128, 128, lambda r, c: (c < HALO) & (r == par * 64 + c // 4))
        spread_w = hot(128, 128, lambda r, c: (c >= 128 - HALO) & (r == par * 64 + 60 + (c - 112) // 4))
        core = mul(cext[0], spread_c)
        edge = mul(cext[1], spread_e) + mul(cext[2], spread_w)
        wide.append(jnp.concatenate([core, edge], axis=1))
    wide = jnp.concatenate(wide, axis=0)
    tall = hot(EXT, 80, lambda r, c: ((r % 8) * STRIP + r // 8) // 4 == 2 * (c % 40) + c // 40)
    fine = mul(tall, wide)
    for c in range(LT):
        part = fine[:, c * 128:(c + 1) * 128].reshape(STRIP, 8, 128)
        if c == 2:
            part = jnp.where(part == 0.0, 1.0, part)
        FR[:, c] = part

    base = float(visc_scale * np.power(strain_floor, -1.0 / 3.0))

    def faces(first, src, last_rows):
        @pl.loop(0, STRIP)
        def _(i):
            if first:
                m = (0.5 * base) * T[i]
            else:
                U, UE, UW, V, VE, VW = src
                ux = 0.5 * (UE[i + 1] - UW[i + 1])
                vx = 0.5 * (VE[i + 1] - VW[i + 1])
                uy = 0.5 * (U[i + 2] - U[i])
                vy = 0.5 * (V[i + 2] - V[i])
                sh = uy + vx
                strain = ux * ux + vy * vy + ux * vy + 0.25 * (sh * sh) + strain_floor
                m = (0.5 * visc_scale) * T[i] * jnp.exp2(jnp.log2(strain) * (-1.0 / 3.0))
            H[i + 1] = m
            A[i] = east(m)
            B[i] = west(m)

        wrap([H])

        @pl.loop(0, STRIP)
        def _(i):
            h = H[i + 1]
            ew = 2.0 * h + A[i] + B[i]
            sn = 2.0 * h + H[i] + H[i + 2]
            fr = FR[i]
            ice = IC[i]
            iu = ice / (fr + 4.0 * ew + sn)
            iv = ice / (fr + ew + 4.0 * sn)
            IU[i] = iu
            IV[i] = iv
            if first:
                put(last_rows, i, iu * FU[i], iv * FV[i])

        if first:
            wrap(last_rows)

    def put(dst, i, u, v):
        U, UE, UW, V, VE, VW = dst
        U[i + 1] = u
        UE[i + 1] = east(u)
        UW[i + 1] = west(u)
        V[i + 1] = v
        VE[i + 1] = east(v)
        VW[i + 1] = west(v)

    def sweep(src, dst, fu_ref, fv_ref):
        U, UE, UW, V, VE, VW = src

        @pl.loop(0, STRIP // UNROLL)
        def _(it):
            b = it * UNROLL
            new_u = [[None] * LT for _ in range(UNROLL)]
            new_v = [[None] * LT for _ in range(UNROLL)]
            n = UNROLL + 2
            for c in range(LT):
                u = [U[b + j, c] for j in range(n)]
                ue = [UE[b + j, c] for j in range(n)]
                uw = [UW[b + j, c] for j in range(n)]
                v = [V[b + j, c] for j in range(n)]
                ve = [VE[b + j, c] for j in range(n)]
                vw = [VW[b + j, c] for j in range(n)]
                h = [H[b + j, c] for j in range(n)]
                q = [h[j] * (ve[j] - vw[j]) for j in range(n)]
                r = [h[j] * (ue[j] - uw[j]) for j in range(n)]
                face = [h[j] + h[j + 1] for j in range(n - 1)]
                for k in range(UNROLL):
                    j = k + 1
                    a = A[b + k, c]
                    w_ = B[b + k, c]
                    fe = h[j] + a
                    fw = h[j] + w_
                    so = face[j]
                    no = face[j - 1]
                    cu = a * (ve[j + 1] - ve[j - 1]) - w_ * (vw[j + 1] - vw[j - 1]) + 0.5 * (q[j + 1] - q[j - 1])
                    cv = 0.5 * (a * (ue[j + 1] - ue[j - 1]) - w_ * (uw[j + 1] - uw[j - 1])) + (r[j + 1] - r[j - 1])
                    tu = fe * ue[j] + fw * uw[j]
                    su = so * u[j + 1] + no * u[j - 1]
                    tv = fe * ve[j] + fw * vw[j]
                    sv = so * v[j + 1] + no * v[j - 1]
                    new_u[k][c] = IU[b + k, c] * (fu_ref[b + k, c] + 4.0 * tu + su + cu)
                    new_v[k][c] = IV[b + k, c] * (fv_ref[b + k, c] + tv + 4.0 * sv + cv)
            for k in range(UNROLL):
                put(dst, b + k, jnp.stack(new_u[k]), jnp.stack(new_v[k]))

        wrap(dst)

    zero = (U0, UE0, UW0, V0, VE0, VW0)
    one = (U1, UE1, UW1, V1, VE1, VW1)
    faces(True, None, one)
    sweep(one, zero, FU, FV)
    for _ in range(1, PIC):
        faces(False, zero, None)
        sweep(zero, one, FU, FV)
        sweep(one, zero, FU, FV)

    @pl.loop(0, STRIP)
    def _(i):
        u = U0[i + 1]
        v = V0[i + 1]
        FU[i] = u
        FV[i] = v
        mu = u - OU[i]
        mv = v - OV[i]
        OU[i] = mu
        OV[i] = mv
        put(one, i, IU[i] * mu, IV[i] * mv)

    wrap(one)
    for out, ref in ((out_u, FU), (out_v, FV)):
        @pl.loop(0, STRIP)
        def _(i):
            for c in range(2):
                nat[c, pl.ds(i, 8, stride=STRIP), :] = ref[i, c]

        for c in range(2):
            out[:, pl.ds(c * 128, 128)] = nat[c, pl.ds(HALO, TILE)]

    src, dst = one, zero
    for _ in range(1, ADJ):
        sweep(src, dst, OU, OV)
        src, dst = dst, src

    @pl.loop(0, STRIP)
    def _(i):
        T[i] = -FR[i] * (FU[i] * src[0][i + 1] + FV[i] * src[3][i + 1])

    cells = jnp.concatenate([T[:, 0].reshape(EXT, 128), T[:, 1].reshape(EXT, 128)], axis=1)
    fold = hot(TILE, 128, lambda r, c: r // 4 == c % 64)
    cols = mul(cells, fold)
    parts = []
    for par in range(2):
        pick = hot(32, EXT, lambda r, c: ((c % 8) * STRIP + c // 8) // 4 - HALO // 4 == 2 * r + par)
        parts.append(mul(pick, cols))
    lanes = lax.broadcasted_iota(jnp.int32, (32, 128), 1)
    grad[...] = jnp.where(lanes < 64, parts[0], parts[1])


def reduce_kernel(
    blk, grad, out,
    tiles, part, slots, red, rows,
    a_send, a_recv, b_send, b_recv, c_send, c_recv,
):
    gx = lax.axis_index("gx")
    gy = lax.axis_index("gy")

    def dev(dy, dx):
        return (lax.rem(gx + dx + GX, GX), lax.rem(gy + dy + GY, GY))

    def remote(src, dst, ss, rs, to):
        return pltpu.make_async_remote_copy(
            src_ref=src, dst_ref=dst, send_sem=ss, recv_sem=rs, device_id=to, device_id_type=MESH
        )

    barrier = pltpu.get_barrier_semaphore()
    peers = [(dy, 0) for dy in range(1, GY)] + [(0, dx) for dx in range(1, GX)]
    for dy, dx in peers:
        pl.semaphore_signal(barrier, inc=1, device_id=dev(dy, dx), device_id_type=MESH)
    pl.semaphore_wait(barrier, len(peers))

    first = [
        remote(grad, tiles.at[off], a_send.at[off], a_recv.at[off], dev(off, 0)) for off in range(1, GY)
    ]
    for c in first:
        c.start()
    tiles[0] = grad[...]
    for c in first:
        c.wait_recv()
    for k in range(4):
        total = jnp.zeros((32, 128), F32)
        for off in range(GY):
            owner = blk[lax.rem(gy - off + GY, GY), gx]
            total = total + jnp.where(owner == 4 * gy + k, tiles[off], 0.0)
        for g in range(GX):
            part[g, pl.ds(4 * k, 4)] = total[4 * g:4 * g + 4]
    second = []
    for off in range(1, GX):
        to = lax.rem(gx + off, GX)
        second.append(remote(part.at[to], slots.at[off], b_send.at[off], b_recv.at[off], dev(0, off)))
    for c in second:
        c.start()
    for c in second:
        c.wait_recv()
    total = part[gx]
    for off in range(1, GX):
        total = total + slots[off]
    red[...] = total
    third = [
        remote(red, rows.at[gx], c_send.at[off], c_recv.at[off], dev(0, off)) for off in range(1, GX)
    ]
    for c in third:
        c.start()
    rows[gx] = total
    for c in third:
        c.wait()
    for c in first + second:
        c.wait_send()
    for g in range(GX):
        for k in range(4):
            out[k, pl.ds(4 * g, 4)] = rows[g, pl.ds(4 * k, 4)]


def vmem(n=None):
    return pl.BlockSpec(memory_space=pltpu.VMEM)


def smem():
    return pl.BlockSpec(memory_space=pltpu.SMEM)


def per_device(thickness, driving, observed, control, ice_mask, tile_block):
    shape = jax.ShapeDtypeStruct
    blocks = tile_block.reshape(GY, GX)
    coarse_in = control.reshape(4, 32, 128)
    dma = pltpu.SemaphoreType.DMA
    h_north, h_south, h_west, h_east, coarse = pl.pallas_call(
        exchange_kernel,
        name="exchange",
        out_shape=(
            shape((5, HALO, TILE), F32),
            shape((5, HALO, TILE), F32),
            shape((EXT, 128), F32),
            shape((EXT, 128), F32),
            shape((9, 32, 128), F32),
        ),
        in_specs=[smem()] + [vmem()] * 4,
        out_specs=[vmem()] * 5,
        scratch_shapes=[
            pltpu.VMEM((TILE, 128), F32),
            pltpu.VMEM((TILE, 128), F32),
            pltpu.VMEM((GY, 32, 128), F32),
            pltpu.VMEM((GY, 32, 128), F32),
            dma((GY,)), dma((GY,)), dma((12,)), dma((12,)), dma((9,)), dma((9,)),
        ],
        compiler_params=pltpu.CompilerParams(collective_id=0, has_side_effects=True),
    )(blocks, thickness, driving, observed, coarse_in)

    field = pltpu.VMEM((STRIP, LT, 8, 128), F32)
    padded = pltpu.VMEM((STRIP + 2, LT, 8, 128), F32)
    vel_u, vel_v, grad = pl.pallas_call(
        solve_kernel,
        name="solve",
        out_shape=(shape((TILE, TILE), F32), shape((TILE, TILE), F32), shape((32, 128), F32)),
        in_specs=[smem()] + [vmem()] * 8,
        out_specs=[vmem()] * 3,
        scratch_shapes=[
            pltpu.VMEM((LT, EXT, 128), F32),
            pltpu.VMEM((3, 40, 128), F32),
            field, field, field, field, field, field, field,
            padded, field, field, field, field,
        ] + [padded] * 12,
        compiler_params=pltpu.CompilerParams(vmem_limit_bytes=40 << 20),
    )(ice_mask, thickness, driving, observed, h_north, h_south, h_west, h_east, coarse)

    total = pl.pallas_call(
        reduce_kernel,
        name="reduce",
        out_shape=shape((4, 32, 128), F32),
        in_specs=[smem(), vmem()],
        out_specs=vmem(),
        scratch_shapes=[
            pltpu.VMEM((GY, 32, 128), F32),
            pltpu.VMEM((GX, 16, 128), F32),
            pltpu.VMEM((GX, 16, 128), F32),
            pltpu.VMEM((16, 128), F32),
            pltpu.VMEM((GX, 16, 128), F32),
            dma((GY,)), dma((GY,)), dma((GX,)), dma((GX,)), dma((GX,)), dma((GX,)),
        ],
        compiler_params=pltpu.CompilerParams(collective_id=1, has_side_effects=True),
    )(blocks, grad)
    return vel_u, vel_v, total.reshape(4, 4096)


def solution(mesh):
    return jax.shard_map(
        per_device,
        mesh=mesh,
        in_specs=(P("gy", "gx"), P(None, "gy", "gx"), P(None, "gy", "gx"), P("gy", None), P(), P()),
        out_specs=(P("gy", "gx"), P("gy", "gx"), P("gy", None)),
        check_vma=False,
    )
```

time: 719 us -> 111 us (0.15); the launches traced: 709 us -> 110 us
  waiting for transfers between devices: 373 us -> 0 us
  starting transfers between devices: 229 us -> 0 us
  Pallas kernels: 0 us -> 99.9 us
  other arithmetic: 48.5 us -> 0 us
  local copies, waits for them, and re-layouts: 37.6 us -> 9.53 us
  between operations: 16.9 us -> 0.7 us
    ppermute x68 -> x0, starting transfers between devices: 229 us -> none  [the longest x34 185 us: with_halo(): lax.ppermute(tail, axis, [(i, (i + 1) % count) for i in range(ends)])]
    unnamed x4 -> x0, waiting for transfers between devices: 188 us -> none
    pallas_call x0 -> x3, Pallas kernels: none -> 99.9 us  [the longest x1 58.4 us: per_device(): pl.pallas_call(solve_kernel, name='solve', out_shape=(shape((TILE, TILE),...]
    ppermute x68 -> x0, waiting for transfers between devices: 89.6 us -> none  [the longest x34 53.8 us: with_halo(): lax.ppermute(head, axis, [((i + 1) % count, i) for i in range(ends)])]
    psum x1 -> x0, waiting for transfers between devices: 75.7 us -> none  [per_device(): gradient = lax.psum(partial_sum, 'gx')]
    mul x50 -> x0, other arithmetic: 20.2 us -> none  [the longest x14 5.95 us: relaxation(): flux_s = visc_pad[1:-1, :] * (0.5 * (speed_x[2:, :] - speed_x[:-2, :]))]
    all_gather x1 -> x0, waiting for transfers between devices: 19.9 us -> none  [per_device(): shard_rows = lax.all_gather(rates, 'gy', axis=0, tiled=True)]
    another operation x37 -> x0, other arithmetic: 16.4 us -> none  [the longest x36 15.8 us: relaxation(): return jnp.stack([new_u, new_v])]
  transfers between devices with their start and end apart: 71 -> 0, of which waited for: 52 -> 0; matrix products, arithmetic and copies ran while one was open for 2% -> 0% of each run, Pallas kernels for 0% -> 0%
where the time goes in v1:
time: 111 us; the launch traced here: 110 us
  Pallas kernels  99.9 us (90%)
  local copies, waits for them, and re-layouts  9.53 us (9%)
    pallas_call x1, Pallas kernels, per_device(): pl.pallas_call(solve_kernel, name='solve', out_shape=(shape((TILE, TILE),...  58.4 us
    pallas_call x1, Pallas kernels, per_device(): pl.pallas_call(exchange_kernel, name='exchange', out_shape=(shape((5, HAL...  22.9 us
    pallas_call x1, Pallas kernels, per_device(): pl.pallas_call(reduce_kernel, name='reduce', out_shape=shape((4, 32, 128)...  18.7 us
    unnamed x23, local copies, waits for them, and re-layouts  8.18 us

profile of v1, /device:TPU:0, one launch (start us, length us, event | category | flops | bytes accessed | tf_op | source)
XLA Modules:
  0.0 110.2 jit_solution(11241763869283447649)
XLA Ops:
  0.6 0.0 copy-start.9
  0.6 1.4 %copy.9.blk = s32[16,8]{1,0:T(8,128)} copy(s32[16,8]{0,1:T(8,128)} %bitcast.13) | data formatting | bytes 1024 | tf_op jit(solution)/shard_map/reshape | solution.py:439
  2.0 0.0 copy-done.9
  2.0 0.1 copy.10.ice_ref
  2.1 1.5 %copy.17 = f32[1,4,32,128]{3,2,1,0:T(8,128)} copy(f32[1,4,32,128]{3,1,2,0:T(4,128)} %bitcast.11) | data formatting | bytes 131072
  3.5 0.0 copy-start
  3.5 0.0 copy-start.1
  3.5 0.0 copy-start.2
  3.6 22.9 %exchange.1 = (f32[5,16,256]{2,1,0:T(8,128)}, f32[5,16,256]{2,1,0:T(8,128)}, f32[288,128]{1,0:T(8,128)}, f32[288,128]{1,0:T(8,128)}, f32[9,32,128]{2,1,0:T(8,128)}) custom-call(s32[16,8]{1,0:T(8,128)} %copy.9.blk, f32[256,256]{1,0:T(8,128)} %thick.3, f32[2,256,256]{2,1,0:T(8,128)} %drv.3, f32[2,256,256]{2,1,0:T(8,128)} %obs.3, f32[4,32,128]{2,1,0:T(8,128)} %bitcast.10), custom_call_target="tpu_custom_call" | custom-call | tf_op jit(solution)/shard_map/exchange/pallas_call | solution.py:442
  26.5 0.0 copy-done
  26.5 0.0 copy-done.1
  26.5 0.0 copy-done.2
  26.5 0.0 copy-start.3
  26.5 0.9 copy-done.3
  27.4 0.0 copy-start.4
  27.4 0.9 copy-done.4
  28.3 0.9 copy-done.5
  29.2 0.9 copy-done.6
  30.1 0.9 copy-done.7
  31.0 58.4 %solve.1 = (f32[256,256]{1,0:T(8,128)}, f32[256,256]{1,0:T(8,128)}, f32[32,128]{1,0:T(8,128)S(1)}) custom-call(s32[16,8]{1,0:T(8,128)S(1)} %copy.10.ice_ref, f32[256,256]{1,0:T(8,128)S(1)} %copy-done.2, f32[2,256,256]{2,1,0:T(8,128)S(1)} %copy-done, f32[2,256,256]{2,1,0:T(8,128)S(1)} %copy-done.1, f32[5,16,256]{2,1,0:T(8,128)S(1)} %copy-done.6, ...), custom_call_target="tpu_custom_call" | custom-call | tf_op jit(solution)/shard_map/solve/pallas_call | solution.py:466
  89.4 0.0 copy-start.8
  89.4 0.6 copy-done.8
  90.0 18.7 %reduce.1 = f32[4,32,128]{2,1,0:T(8,128)} custom-call(s32[16,8]{1,0:T(8,128)} %copy.9.blk, f32[32,128]{1,0:T(8,128)} %copy-done.8), custom_call_target="tpu_custom_call" | custom-call | tf_op jit(solution)/shard_map/reduce/pallas_call | solution.py:481
  108.7 1.5 %copy.16 = f32[1,4,32,128]{3,1,2,0:T(4,128)} copy(f32[1,4,32,128]{3,2,1,0:T(8,128)} %bitcast.9) | data formatting | bytes 131072
  (3 shorter events, 0.0 us)
Async XLA Ops:
  0.6 1.4 %copy-start.9 = (s32[16,8]{0,1:T(8,128)S(1)}, s32[16,8]{0,1:T(8,128)}, u32[]{:S(2)}) copy-start(s32[16,8]{0,1:T(8,128)} %param.10) | copy-start | bytes 1540
  3.5 22.9 %copy-start = (f32[2,256,256]{2,1,0:T(8,128)S(1)}, f32[2,256,256]{2,1,0:T(8,128)}, u32[]{:S(2)}) copy-start(f32[2,256,256]{2,1,0:T(8,128)} %drv.3) | copy-start | bytes 1572868
  3.5 22.9 %copy-start.1 = (f32[2,256,256]{2,1,0:T(8,128)S(1)}, f32[2,256,256]{2,1,0:T(8,128)}, u32[]{:S(2)}) copy-start(f32[2,256,256]{2,1,0:T(8,128)} %obs.3) | copy-start | bytes 1572868
  3.5 22.9 %copy-start.2 = (f32[256,256]{1,0:T(8,128)S(1)}, f32[256,256]{1,0:T(8,128)}, u32[]{:S(2)}) copy-start(f32[256,256]{1,0:T(8,128)} %thick.3) | copy-start | bytes 786436
  26.5 0.9 copy-start.3
  27.4 0.9 copy-start.4
  28.3 0.9 copy-start.5
  29.2 0.9 copy-start.6
  30.1 0.9 copy-start.7
  89.4 0.6 copy-start.8

commit v2 on v0

v2 whole, which is shorter than its diff:
```python
import jax
import jax.numpy as jnp
import numpy as np
from jax import lax
from jax.experimental import pallas as pl
from jax.experimental.pallas import tpu as pltpu
from jax.sharding import PartitionSpec as P

TILE = 256
HALO = 16
EXT = TILE + 2 * HALO
STRIP = EXT // 8
GROUP = STRIP // 4
LT = 3
PIC = 4
ADJ = 6
GX = 8
GY = 16
ROWS = 12
MROWS = 12
REMOTE = True
MESH = pl.DeviceIdType.MESH
F32 = jnp.float32

visc_scale = 0.1
strain_floor = 0.05


def kernel(
    blk, ice_ref, thick, drv, obs, ctl,
    out_u, out_v, out_g,
    nat, pack_w, pack_e, h_west, h_east, c_send, c_recv, coarse, cext,
    T, FU, FV, OU, OV, FR, IC, H, A, B, IU, IV,
    U0, UE0, UW0, V0, VE0, VW0, U1, UE1, UW1, V1, VE1, VW1,
    small, grad, tiles, part, slots, red, gathered,
    l_sem, o_sem, g_send, g_recv, x_send, x_recv, n_send, n_recv,
    a_send, a_recv, b_send, b_recv, d_send, d_recv,
):
    gx = lax.axis_index("gx")
    gy = lax.axis_index("gy")

    def dev(dy, dx):
        return (lax.rem(gx + dx + GX, GX), lax.rem(gy + dy + GY, GY))

    def remote(src, dst, ss, rs, to):
        return pltpu.make_async_remote_copy(
            src_ref=src, dst_ref=dst, send_sem=ss, recv_sem=rs, device_id=to, device_id_type=MESH
        )

    near = [(dy, dx) for dy in (-1, 0, 1) for dx in (-1, 0, 1) if (dy, dx) != (0, 0)]
    if REMOTE:
        barrier = pltpu.get_barrier_semaphore()
        peers = [(dy, 0) for dy in range(1, GY)] + [(0, dx) for dx in range(1, GX)]
        peers += [(dy, dx) for dy, dx in near if dy * dx]
        for dy, dx in peers:
            pl.semaphore_signal(barrier, inc=1, device_id=dev(dy, dx), device_id_type=MESH)

    inner = pl.ds(HALO, TILE)
    loads = []
    for f, src in enumerate((thick, drv.at[0], drv.at[1], obs.at[0], obs.at[1])):
        for c in range(2):
            loads.append(
                pltpu.make_async_copy(src.at[:, pl.ds(c * 128, 128)], nat.at[f, c, inner], l_sem.at[f, c])
            )
    for copy in loads:
        copy.start()

    for off in range(GY):
        c_send[off] = ctl[lax.rem(blk[lax.rem(gy + off, GY), gx], 4)]
    c_recv[0] = c_send[0]

    lane = lax.broadcasted_iota(jnp.int32, (8, 128), 1)
    sub = lax.broadcasted_iota(jnp.int32, (8, 128), 0)
    lane3 = lax.broadcasted_iota(jnp.int32, (LT, 8, 128), 2)

    gathers, halos, spread = [], [], []
    if REMOTE:
        pl.semaphore_wait(barrier, len(peers))
        gathers = [
            remote(c_send.at[off], c_recv.at[off], g_send.at[off], g_recv.at[off], dev(off, 0))
            for off in range(1, GY)
        ]
        for g in gathers:
            g.start()
    for copy in loads:
        copy.wait()
    if REMOTE:
        moves = [
            (nat.at[:, :, pl.ds(TILE, HALO)], nat.at[:, :, pl.ds(0, HALO)], (1, 0)),
            (nat.at[:, :, pl.ds(HALO, HALO)], nat.at[:, :, pl.ds(HALO + TILE, HALO)], (-1, 0)),
        ]
        halos = [remote(s, d, x_send.at[n], x_recv.at[n], dev(*to)) for n, (s, d, to) in enumerate(moves)]
        for h in halos:
            h.start()

    @pl.loop(0, TILE // 32)
    def _(t):
        for k in range(4):
            rows = pl.ds(pl.multiple_of(t * 32, 32) + 8 * k, 8)
            src = pl.ds(pl.multiple_of(t * 32, 32) + 8 * k + HALO, 8)
            w = nat[0, 0, src]
            e = nat[0, 1, src]
            for f in range(1, 5):
                w = jnp.where(lane < 16 * f, w, pltpu.roll(nat[f, 0, src], 16 * f, 1))
                e = jnp.where(lane >= 128 - 16 * f, e, pltpu.roll(nat[f, 1, src], 128 - 16 * f, 1))
            pack_w[rows, :] = w
            pack_e[rows, :] = e

    if REMOTE:
        lo, hi = pl.ds(0, HALO), pl.ds(TILE - HALO, HALO)
        first, last = pl.ds(0, HALO), pl.ds(TILE + HALO, HALO)
        moves = [
            (pack_e, h_west.at[inner], (0, 1)),
            (pack_w, h_east.at[inner], (0, -1)),
            (pack_e.at[hi], h_west.at[first], (1, 1)),
            (pack_e.at[lo], h_west.at[last], (-1, 1)),
            (pack_w.at[hi], h_east.at[first], (1, -1)),
            (pack_w.at[lo], h_east.at[last], (-1, -1)),
        ]
        sides = [
            remote(s, d, x_send.at[n + 2], x_recv.at[n + 2], dev(*to)) for n, (s, d, to) in enumerate(moves)
        ]
        for h in sides:
            h.start()
        halos = halos + sides
        for g in gathers:
            g.wait_recv()
    coarse[4] = c_recv[lax.rem(gy - blk[gy, gx] // 4 + GY, GY)]
    if REMOTE:
        for dy, dx in near:
            slot = (1 - dy) * 3 + (1 - dx)
            spread.append(remote(coarse.at[4], coarse.at[slot], n_send.at[slot], n_recv.at[slot], dev(dy, dx)))
        for n in spread:
            n.start()

    inside, iced = {}, {}
    for dy, dx in near + [(0, 0)]:
        ok = (gy + dy >= 0) & (gy + dy < GY) & (gx + dx >= 0) & (gx + dx < GX)
        flag = jnp.where(ok, 1.0, 0.0)
        at = ice_ref[jnp.clip(gy + dy, 0, GY - 1), jnp.clip(gx + dx, 0, GX - 1)]
        inside[dy, dx] = flag
        iced[dy, dx] = flag * at.astype(F32)

    def region(cls, table):
        def by_row(dx):
            mid = jnp.full((8, 128), table[0, dx], F32)
            if cls == 0:
                return jnp.where(sub == 0, table[-1, dx], mid)
            if cls == 2:
                return jnp.where(sub == 7, table[1, dx], mid)
            return mid

        center = by_row(0)
        edge = jnp.where(lane < HALO, by_row(1), jnp.where(lane >= 128 - HALO, by_row(-1), 0.0))
        return jnp.stack([center, center, edge])

    for cls in range(3):
        IC[cls] = region(cls, iced)

    def west(x):
        y = pltpu.roll(x, 1, 2)
        return jnp.where(lane3 == 0, jnp.concatenate([y[2:], y[:2]], axis=0), y)

    def east(x):
        y = pltpu.roll(x, 127, 2)
        return jnp.where(lane3 == 127, jnp.concatenate([y[1:], y[:1]], axis=0), y)

    def wrap(refs):
        for ref in refs:
            ref[0] = pltpu.roll(ref[STRIP], 1, 1)
            ref[STRIP + 1] = pltpu.roll(ref[1], 7, 1)

    for h in halos:
        h.wait()

    keep = [region(cls, inside) for cls in range(3)]
    for i in range(STRIP):
        at = pl.ds(i, 8, stride=STRIP)
        right = h_east[at, :]
        left = h_west[at, :]
        cls = 0 if i < 16 else (1 if i < 20 else 2)
        for f, dst in enumerate((T, FU, FV, OU, OV)):
            r = pltpu.roll(right, 128 - 16 * f, 1) if f else right
            l = pltpu.roll(left, 16 * f, 1) if f else left
            edge = jnp.where(lane < HALO, r, jnp.where(lane >= 128 - HALO, l, 0.0))
            x = jnp.stack([nat[f, 0, at, :], nat[f, 1, at, :], edge])
            if f == 0:
                x = jnp.where(keep[cls] > 0.0, x, 0.0)
            dst[i] = x

    for n in spread:
        n.wait_recv()
    for g, dx in enumerate((0, 1, -1)):
        flat = jnp.concatenate(
            [coarse[1 + dx, pl.ds(24, 8)], coarse[4 + dx], coarse[7 + dx, pl.ds(0, 8)]], axis=0
        )
        flat = jnp.exp(flat)
        cext[g, pl.ds(0, 48, stride=2), :] = flat
        cext[g, pl.ds(1, 48, stride=2), :] = pltpu.roll(flat, 64, 1)
    quarter = lane // 4
    for i in range(GROUP):
        at = pl.ds(12 + i, 8, stride=GROUP)
        mid, right, left = (cext[g, at, :] for g in range(3))
        edges = jnp.where(lane < 64, right, pltpu.roll(left, 64, 1))
        t0 = jnp.take_along_axis(mid, quarter, axis=1)
        t1 = jnp.take_along_axis(mid, quarter + 32, axis=1)
        t2 = jnp.take_along_axis(edges, jnp.where(lane < 64, quarter, 96 + quarter), axis=1)
        FR[i] = jnp.stack([t0, t1, t2])

    base = float(visc_scale * np.power(strain_floor, -1.0 / 3.0))

    def put(dst, i, u, v):
        U, UE, UW, V, VE, VW = dst
        U[i + 1] = u
        UE[i + 1] = east(u)
        UW[i + 1] = west(u)
        V[i + 1] = v
        VE[i + 1] = east(v)
        VW[i + 1] = west(v)

    def viscosity(src):
        @pl.loop(0, STRIP // MROWS)
        def _(it):
            for k in range(MROWS):
                i = it * MROWS + k
                if src is None:
                    m = (0.5 * base) * T[i]
                else:
                    U, UE, UW, V, VE, VW = src
                    ux = 0.5 * (UE[i + 1] - UW[i + 1])
                    vx = 0.5 * (VE[i + 1] - VW[i + 1])
                    uy = 0.5 * (U[i + 2] - U[i])
                    vy = 0.5 * (V[i + 2] - V[i])
                    sh = uy + vx
                    strain = ux * ux + vy * vy + ux * vy + 0.25 * (sh * sh) + strain_floor
                    m = (0.5 * visc_scale) * T[i] * jnp.exp2(jnp.log2(strain) * (-1.0 / 3.0))
                H[i + 1] = m
                A[i] = east(m)
                B[i] = west(m)

        wrap([H])

    def sweep(src, dst, fu_ref, fv_ref, fresh):
        @pl.loop(0, STRIP // ROWS)
        def _(it):
            b = it * ROWS
            new_u = [[None] * LT for _ in range(ROWS)]
            new_v = [[None] * LT for _ in range(ROWS)]
            n = ROWS + 2
            for c in range(LT):
                h = [H[b + j, c] for j in range(n)]
                face = [h[j] + h[j + 1] for j in range(n - 1)]
                if src is not None:
                    u, ue, uw, v, ve, vw = ([ref[b + j, c] for j in range(n)] for ref in src)
                    q = [h[j] * (ve[j] - vw[j]) for j in range(n)]
                    r = [h[j] * (ue[j] - uw[j]) for j in range(n)]
                for k in range(ROWS):
                    j = k + 1
                    i = b + k
                    a = A[i, c]
                    w_ = B[i, c]
                    fe = h[j] + a
                    fw = h[j] + w_
                    so = face[j]
                    no = face[j - 1]
                    if fresh:
                        ew = fe + fw
                        sn = so + no
                        fr = FR[it * (ROWS // 4) + k // 4, c]
                        step = i // 4
                        cls = jnp.where(step < 4, 0, jnp.where(step < 5, 1, 2))
                        ice = IC[cls, c]
                        if c == 2:
                            fr = jnp.where(ice > 0.0, fr, 1.0)
                        iu = ice / (fr + 4.0 * ew + sn)
                        iv = ice / (fr + ew + 4.0 * sn)
                        IU[i, c] = iu
                        IV[i, c] = iv
                    else:
                        iu = IU[i, c]
                        iv = IV[i, c]
                    fu = fu_ref[i, c]
                    fv = fv_ref[i, c]
                    if src is not None:
                        cu = a * (ve[j + 1] - ve[j - 1]) - w_ * (vw[j + 1] - vw[j - 1]) + 0.5 * (q[j + 1] - q[j - 1])
                        cv = 0.5 * (a * (ue[j + 1] - ue[j - 1]) - w_ * (uw[j + 1] - uw[j - 1])) + (r[j + 1] - r[j - 1])
                        tu = fe * ue[j] + fw * uw[j]
                        su = so * u[j + 1] + no * u[j - 1]
                        tv = fe * ve[j] + fw * vw[j]
                        sv = so * v[j + 1] + no * v[j - 1]
                        fu = fu + 4.0 * tu + su + cu
                        fv = fv + tv + 4.0 * sv + cv
                    new_u[k][c] = iu * fu
                    new_v[k][c] = iv * fv
            for k in range(ROWS):
                put(dst, b + k, jnp.stack(new_u[k]), jnp.stack(new_v[k]))

        wrap(dst)

    zero = (U0, UE0, UW0, V0, VE0, VW0)
    one = (U1, UE1, UW1, V1, VE1, VW1)
    viscosity(None)
    sweep(None, one, FU, FV, True)
    sweep(one, zero, FU, FV, False)

    @pl.loop(1, PIC)
    def _(_):
        viscosity(zero)
        sweep(zero, one, FU, FV, True)
        sweep(one, zero, FU, FV, False)

    @pl.loop(0, STRIP // 4)
    def _(it):
        for k in range(4):
            i = it * 4 + k
            u = U0[i + 1]
            v = V0[i + 1]
            FU[i] = u
            FV[i] = v
            at = pl.ds(i, 8, stride=STRIP)
            for c in range(2):
                nat[0, c, at, :] = u[c]
                nat[1, c, at, :] = v[c]
            mu = u - OU[i]
            mv = v - OV[i]
            OU[i] = mu
            OV[i] = mv
            put(one, i, IU[i] * mu, IV[i] * mv)

    stores = []
    for f, dst in enumerate((out_u, out_v)):
        for c in range(2):
            stores.append(
                pltpu.make_async_copy(nat.at[f, c, inner], dst.at[:, pl.ds(c * 128, 128)], o_sem.at[f, c])
            )
    for s in stores:
        s.start()
    wrap(one)

    @pl.loop(0, (ADJ - 2) // 2)
    def _(_):
        sweep(one, zero, OU, OV, False)
        sweep(zero, one, OU, OV, False)

    sweep(one, zero, OU, OV, False)

    for i in range(GROUP):
        total = None
        for k in range(4):
            j = i * 4 + k
            cell = [FU[j, c] * U0[j + 1, c] + FV[j, c] * V0[j + 1, c] for c in range(2)]
            total = cell if total is None else [total[c] + cell[c] for c in range(2)]
        spots = []
        for c in range(2):
            x = -FR[i, c] * total[c]
            x = x + pltpu.roll(x, 127, 1)
            x = x + pltpu.roll(x, 126, 1)
            spots.append(jnp.take_along_axis(x, (lane % 32) * 4, axis=1))
        both = jnp.where(lane % 64 < 32, spots[0], spots[1])
        small[pl.ds(i, 8, stride=GROUP), :] = both
    even = small[pl.ds(4, 32, stride=2), :]
    odd = small[pl.ds(5, 32, stride=2), :]
    wide = lax.broadcasted_iota(jnp.int32, (32, 128), 1)
    grad[...] = jnp.where(wide < 64, even, odd)

    first, second, third = [], [], []
    if REMOTE:
        first = [
            remote(grad, tiles.at[off], a_send.at[off], a_recv.at[off], dev(off, 0)) for off in range(1, GY)
        ]
    for c in first:
        c.start()
    tiles[0] = grad[...]
    for c in first:
        c.wait_recv()
    for k in range(4):
        total = jnp.zeros((32, 128), F32)
        for off in range(GY):
            owner = blk[lax.rem(gy - off + GY, GY), gx]
            total = total + jnp.where(owner == 4 * gy + k, tiles[off], 0.0)
        for g in range(GX):
            part[g, pl.ds(4 * k, 4)] = total[4 * g:4 * g + 4]
    if REMOTE:
        for off in range(1, GX):
            to = lax.rem(gx + off, GX)
            second.append(remote(part.at[to], slots.at[off], b_send.at[off], b_recv.at[off], dev(0, off)))
    for c in second:
        c.start()
    for c in second:
        c.wait_recv()
    total = part[gx]
    for off in range(1, GX):
        total = total + slots[off]
    red[...] = total
    if REMOTE:
        third = [
            remote(red, gathered.at[gx], d_send.at[off], d_recv.at[off], dev(0, off)) for off in range(1, GX)
        ]
    for c in third:
        c.start()
    gathered[gx] = total
    for c in third:
        c.wait()
    for g in range(GX):
        for k in range(4):
            out_g[k, pl.ds(4 * g, 4)] = gathered[g, pl.ds(4 * k, 4)]
    for c in gathers + spread + first + second:
        c.wait_send()
    for s in stores:
        s.wait()


def call(*operands):
    shape = jax.ShapeDtypeStruct
    dma = pltpu.SemaphoreType.DMA
    anywhere = pl.BlockSpec(memory_space=pl.ANY)
    smem = pl.BlockSpec(memory_space=pltpu.SMEM)
    vmem = pl.BlockSpec(memory_space=pltpu.VMEM)
    field = pltpu.VMEM((STRIP, LT, 8, 128), F32)
    padded = pltpu.VMEM((STRIP + 2, LT, 8, 128), F32)
    flat = pltpu.VMEM((32, 128), F32)
    return pl.pallas_call(
        kernel,
        name="friction_gradient",
        out_shape=(shape((TILE, TILE), F32), shape((TILE, TILE), F32), shape((4, 32, 128), F32)),
        in_specs=[smem, smem, anywhere, anywhere, anywhere, vmem],
        out_specs=[anywhere, anywhere, vmem],
        scratch_shapes=[
            pltpu.VMEM((5, 2, EXT, 128), F32),
            pltpu.VMEM((TILE, 128), F32),
            pltpu.VMEM((TILE, 128), F32),
            pltpu.VMEM((EXT, 128), F32),
            pltpu.VMEM((EXT, 128), F32),
            pltpu.VMEM((GY, 32, 128), F32),
            pltpu.VMEM((GY, 32, 128), F32),
            pltpu.VMEM((9, 32, 128), F32),
            pltpu.VMEM((3, 96, 128), F32),
            field, field, field, field, field,
            pltpu.VMEM((GROUP, LT, 8, 128), F32),
            pltpu.VMEM((3, LT, 8, 128), F32),
            padded, field, field, field, field,
        ] + [padded] * 12 + [
            pltpu.VMEM((72, 128), F32),
            flat,
            pltpu.VMEM((GY, 32, 128), F32),
            pltpu.VMEM((GX, 16, 128), F32),
            pltpu.VMEM((GX, 16, 128), F32),
            pltpu.VMEM((16, 128), F32),
            pltpu.VMEM((GX, 16, 128), F32),
            dma((5, 2)), dma((2, 2)),
            dma((GY,)), dma((GY,)), dma((8,)), dma((8,)), dma((9,)), dma((9,)),
            dma((GY,)), dma((GY,)), dma((GX,)), dma((GX,)), dma((GX,)), dma((GX,)),
        ],
        compiler_params=pltpu.CompilerParams(
            vmem_limit_bytes=48 << 20,
            **(dict(collective_id=0, has_side_effects=True) if REMOTE else {}),
        ),
    )(*operands)


def per_device(thickness, driving, observed, control, ice_mask, tile_block):
    vel_u, vel_v, total = call(
        tile_block.reshape(GY, GX), ice_mask, thickness, driving, observed, control.reshape(4, 32, 128)
    )
    return vel_u, vel_v, total.reshape(4, 4096)


def solution(mesh):
    return jax.shard_map(
        per_device,
        mesh=mesh,
        in_specs=(P("gy", "gx"), P(None, "gy", "gx"), P(None, "gy", "gx"), P("gy", None), P(), P()),
        out_specs=(P("gy", "gx"), P("gy", "gx"), P("gy", None)),
        check_vma=False,
    )
```

time: 719 us -> 61.2 us (0.09); the launches traced: 709 us -> 60.9 us
  waiting for transfers between devices: 373 us -> 0 us
  starting transfers between devices: 229 us -> 0 us
  Pallas kernels: 0 us -> 53.5 us
  other arithmetic: 48.5 us -> 0 us
  local copies, waits for them, and re-layouts: 37.6 us -> 6.79 us
  between operations: 16.9 us -> 0.65 us
    ppermute x68 -> x0, starting transfers between devices: 229 us -> none  [the longest x34 185 us: with_halo(): lax.ppermute(tail, axis, [(i, (i + 1) % count) for i in range(ends)])]
    unnamed x4 -> x0, waiting for transfers between devices: 188 us -> none
    ppermute x68 -> x0, waiting for transfers between devices: 89.6 us -> none  [the longest x34 53.8 us: with_halo(): lax.ppermute(head, axis, [((i + 1) % count, i) for i in range(ends)])]
    psum x1 -> x0, waiting for transfers between devices: 75.7 us -> none  [per_device(): gradient = lax.psum(partial_sum, 'gx')]
    pallas_call x0 -> x1, Pallas kernels: none -> 53.5 us  [call(): pl.pallas_call(kernel, name='friction_gradient', out_shape=(shape((TILE,...]
    mul x50 -> x0, other arithmetic: 20.2 us -> none  [the longest x14 5.95 us: relaxation(): flux_s = visc_pad[1:-1, :] * (0.5 * (speed_x[2:, :] - speed_x[:-2, :]))]
    all_gather x1 -> x0, waiting for transfers between devices: 19.9 us -> none  [per_device(): shard_rows = lax.all_gather(rates, 'gy', axis=0, tiled=True)]
    another operation x37 -> x0, other arithmetic: 16.4 us -> none  [the longest x36 15.8 us: relaxation(): return jnp.stack([new_u, new_v])]
  transfers between devices with their start and end apart: 71 -> 0, of which waited for: 52 -> 0; matrix products, arithmetic and copies ran while one was open for 2% -> 0% of each run, Pallas kernels for 0% -> 0%
where the time goes in v2:
time: 61.2 us; the launch traced here: 60.9 us
  Pallas kernels  53.5 us (87%)
  local copies, waits for them, and re-layouts  6.79 us (11%)
  between operations  0.65 us (1%)
    pallas_call x1, Pallas kernels, call(): pl.pallas_call(kernel, name='friction_gradient', out_shape=(shape((TILE,...  53.5 us
    unnamed x13, local copies, waits for them, and re-layouts  6.72 us

profile of v2, /device:TPU:0, one launch (start us, length us, event | category | flops | bytes accessed | tf_op | source)
XLA Modules:
  0.0 60.9 jit_solution(5976801289983401124)
XLA Ops:
  0.6 0.0 copy-start.3
  0.6 0.8 %copy.10.ice_ref = s32[16,8]{1,0:T(8,128)S(1)} copy(s32[16,8]{0,1:T(8,128)} %param.10) | data formatting | bytes 1024 | tf_op args[4]
  1.4 0.0 copy-done.3
  1.4 0.1 copy.9.blk
  1.5 0.8 %copy.16 = f32[1,4,32,128]{3,2,1,0:T(8,128)S(1)} copy(f32[1,4,32,128]{3,1,2,0:T(4,128)} %bitcast.11) | data formatting | bytes 131072
  2.3 0.0 copy-start
  2.3 1.0 %copy-done = f32[2,256,256]{2,1,0:T(8,128)S(1)} copy-done((f32[2,256,256]{2,1,0:T(8,128)S(1)}, f32[2,256,256]{2,1,0:T(8,128)}, u32[]{:S(2)}) %copy-start) | copy-done | bytes 524312
  3.4 0.0 copy-start.1
  3.4 1.0 %copy-done.1 = f32[2,256,256]{2,1,0:T(8,128)S(1)} copy-done((f32[2,256,256]{2,1,0:T(8,128)S(1)}, f32[2,256,256]{2,1,0:T(8,128)}, u32[]{:S(2)}) %copy-start.1) | copy-done | bytes 524312
  4.4 0.0 copy-start.2
  4.4 0.9 %copy-done.2 = f32[256,256]{1,0:T(8,128)S(1)} copy-done((f32[256,256]{1,0:T(8,128)S(1)}, f32[256,256]{1,0:T(8,128)}, u32[]{:S(2)}) %copy-start.2) | copy-done | bytes 262168
  5.4 53.5 %friction_gradient.1 = (f32[256,256]{1,0:T(8,128)S(1)}, f32[256,256]{1,0:T(8,128)S(1)}, f32[4,32,128]{2,1,0:T(8,128)S(1)}) custom-call(s32[16,8]{1,0:T(8,128)S(1)} %copy.9.blk, s32[16,8]{1,0:T(8,128)S(1)} %copy.10.ice_ref, f32[256,256]{1,0:T(8,128)S(1)} %copy-done.2, f32[2,256,256]{2,1,0:T(8,128)S(1)} %copy-done, f32[2,256,256]{2,1,0:T(8,128)S(1)} %copy-done.1, ...), custom_call_target="tpu_custom_call" | custom-call | tf_op jit(solution)/shard_map/friction_gradient/pallas_call | solution.py:422
  58.8 0.7 %copy.15 = f32[1,4,32,128]{3,1,2,0:T(4,128)} copy(f32[1,4,32,128]{3,2,1,0:T(8,128)S(1)} %bitcast.10) | data formatting | bytes 131072
  59.5 0.7 %copy.19 = f32[256,256]{1,0:T(8,128)} copy(f32[256,256]{1,0:T(8,128)S(1)} %get-tuple-element.12) | data formatting | bytes 524288
  60.2 0.7 %copy.20 = f32[256,256]{1,0:T(8,128)} copy(f32[256,256]{1,0:T(8,128)S(1)} %get-tuple-element.13) | data formatting | bytes 524288
Async XLA Ops:
  0.6 0.8 %copy-start.3 = (s32[16,8,1]{0,2,1:T(1,128)S(1)}, s32[16,8,1]{0,2,1:T(1,128)}, u32[]{:S(2)}) copy-start(s32[16,8,1]{0,2,1:T(1,128)} %param.11) | copy-start | bytes 1540
  2.3 1.0 %copy-start = (f32[2,256,256]{2,1,0:T(8,128)S(1)}, f32[2,256,256]{2,1,0:T(8,128)}, u32[]{:S(2)}) copy-start(f32[2,256,256]{2,1,0:T(8,128)} %drv.1) | copy-start | bytes 1572868
  3.4 1.0 %copy-start.1 = (f32[2,256,256]{2,1,0:T(8,128)S(1)}, f32[2,256,256]{2,1,0:T(8,128)}, u32[]{:S(2)}) copy-start(f32[2,256,256]{2,1,0:T(8,128)} %obs.1) | copy-start | bytes 1572868
  4.4 0.9 %copy-start.2 = (f32[256,256]{1,0:T(8,128)S(1)}, f32[256,256]{1,0:T(8,128)}, u32[]{:S(2)}) copy-start(f32[256,256]{1,0:T(8,128)} %thick.1) | copy-start | bytes 786436

commit v3 on v2

--- a/solution.py
+++ b/solution.py
@@ -16,8 +16,8 @@
 ADJ = 6
 GX = 8
 GY = 16
-ROWS = 12
-MROWS = 12
+ROWS = 36
+MROWS = 36
 REMOTE = True
 MESH = pl.DeviceIdType.MESH
 F32 = jnp.float32
@@ -29,11 +29,11 @@
 def kernel(
     blk, ice_ref, thick, drv, obs, ctl,
     out_u, out_v, out_g,
-    nat, pack_w, pack_e, h_west, h_east, c_send, c_recv, coarse, cext,
+    nat, pack_w, pack_e, h_west, h_east, c_in, c_own, c_send, c_recv, coarse, cext,
     T, FU, FV, OU, OV, FR, IC, H, A, B, IU, IV,
     U0, UE0, UW0, V0, VE0, VW0, U1, UE1, UW1, V1, VE1, VW1,
-    small, grad, tiles, part, slots, red, gathered,
-    l_sem, o_sem, g_send, g_recv, x_send, x_recv, n_send, n_recv,
+    small, grad, sums, tiles, part, slots, red, gathered,
+    k_sem, l_sem, o_sem, g_send, g_recv, x_send, x_recv, n_send, n_recv,
     a_send, a_recv, b_send, b_recv, d_send, d_recv,
 ):
     gx = lax.axis_index("gx")
@@ -54,6 +54,9 @@
         peers += [(dy, dx) for dy, dx in near if dy * dx]
         for dy, dx in peers:
             pl.semaphore_signal(barrier, inc=1, device_id=dev(dy, dx), device_id_type=MESH)
+
+    rates = pltpu.make_async_copy(ctl, c_in, k_sem)
+    rates.start()
 
     inner = pl.ds(HALO, TILE)
     loads = []
@@ -65,13 +68,41 @@
     for copy in loads:
         copy.start()
 
-    for off in range(GY):
-        c_send[off] = ctl[lax.rem(blk[lax.rem(gy + off, GY), gx], 4)]
-    c_recv[0] = c_send[0]
-
     lane = lax.broadcasted_iota(jnp.int32, (8, 128), 1)
     sub = lax.broadcasted_iota(jnp.int32, (8, 128), 0)
     lane3 = lax.broadcasted_iota(jnp.int32, (LT, 8, 128), 2)
+
+    rates.wait()
+    for t in range(32):
+        x = c_in[:, pl.ds(t * 128, 128)]
+        for k in range(4):
+            c_own[k, pl.ds(t, 1)] = x[k:k + 1]
+    for off in range(GY):
+        c_send[off] = c_own[lax.rem(blk[gx, 0, lax.rem(gy + off, GY)], 4)]
+    c_recv[0] = c_send[0]
+
+    for f in (3, 4):
+        for c in range(2):
+            nat[f, c, pl.ds(0, 8)] = jnp.zeros((8, 128), F32)
+            nat[f, c, pl.ds(EXT - 8, 8)] = jnp.zeros((8, 128), F32)
+    for copy in loads:
+        copy.wait()
+    shifts = (0, 16, 32, 48, 56)
+    for t in range(16):
+        w = e = None
+        for half in range(2):
+            at = pl.ds(HALO + half * 128 + t * 8, 8)
+            for f in range(5):
+                shift = shifts[f] + 64 * half
+                x = nat[f, 0, at]
+                y = nat[f, 1, at]
+                if shift:
+                    x = pltpu.roll(x, shift, 1)
+                    y = pltpu.roll(y, 128 - shift, 1)
+                w = x if w is None else jnp.where(lane < shift, w, x)
+                e = y if e is None else jnp.where(lane >= 128 - shift, e, y)
+        pack_w[pl.ds(t * 8, 8), :] = w
+        pack_e[pl.ds(t * 8, 8), :] = e
 
     gathers, halos, spread = [], [], []
     if REMOTE:
@@ -80,56 +111,35 @@
             remote(c_send.at[off], c_recv.at[off], g_send.at[off], g_recv.at[off], dev(off, 0))
             for off in range(1, GY)
         ]
-        for g in gathers:
-            g.start()
-    for copy in loads:
-        copy.wait()
-    if REMOTE:
+        main, obs2 = pl.ds(0, 3), pl.ds(3, 2)
+        half = pl.ds(HALO, 128)
+        head, tail = pl.ds(0, HALO), pl.ds(112, HALO)
+        first, last = pl.ds(0, HALO), pl.ds(TILE + HALO, HALO)
         moves = [
-            (nat.at[:, :, pl.ds(TILE, HALO)], nat.at[:, :, pl.ds(0, HALO)], (1, 0)),
-            (nat.at[:, :, pl.ds(HALO, HALO)], nat.at[:, :, pl.ds(HALO + TILE, HALO)], (-1, 0)),
+            (pack_e, h_west.at[half], (0, 1)),
+            (pack_w, h_east.at[half], (0, -1)),
+            (nat.at[main, :, pl.ds(TILE, HALO)], nat.at[main, :, first], (1, 0)),
+            (nat.at[main, :, pl.ds(HALO, HALO)], nat.at[main, :, last], (-1, 0)),
+            (pack_e.at[tail], h_west.at[first], (1, 1)),
+            (pack_e.at[head], h_west.at[last], (-1, 1)),
+            (pack_w.at[tail], h_east.at[first], (1, -1)),
+            (pack_w.at[head], h_east.at[last], (-1, -1)),
+            (nat.at[obs2, :, pl.ds(TILE + 8, 8)], nat.at[obs2, :, pl.ds(8, 8)], (1, 0)),
+            (nat.at[obs2, :, pl.ds(HALO, 8)], nat.at[obs2, :, pl.ds(TILE + HALO, 8)], (-1, 0)),
         ]
         halos = [remote(s, d, x_send.at[n], x_recv.at[n], dev(*to)) for n, (s, d, to) in enumerate(moves)]
-        for h in halos:
-            h.start()
-
-    @pl.loop(0, TILE // 32)
-    def _(t):
-        for k in range(4):
-            rows = pl.ds(pl.multiple_of(t * 32, 32) + 8 * k, 8)
-            src = pl.ds(pl.multiple_of(t * 32, 32) + 8 * k + HALO, 8)
-            w = nat[0, 0, src]
-            e = nat[0, 1, src]
-            for f in range(1, 5):
-                w = jnp.where(lane < 16 * f, w, pltpu.roll(nat[f, 0, src], 16 * f, 1))
-                e = jnp.where(lane >= 128 - 16 * f, e, pltpu.roll(nat[f, 1, src], 128 - 16 * f, 1))
-            pack_w[rows, :] = w
-            pack_e[rows, :] = e
-
-    if REMOTE:
-        lo, hi = pl.ds(0, HALO), pl.ds(TILE - HALO, HALO)
-        first, last = pl.ds(0, HALO), pl.ds(TILE + HALO, HALO)
-        moves = [
-            (pack_e, h_west.at[inner], (0, 1)),
-            (pack_w, h_east.at[inner], (0, -1)),
-            (pack_e.at[hi], h_west.at[first], (1, 1)),
-            (pack_e.at[lo], h_west.at[last], (-1, 1)),
-            (pack_w.at[hi], h_east.at[first], (1, -1)),
-            (pack_w.at[lo], h_east.at[last], (-1, -1)),
-        ]
-        sides = [
-            remote(s, d, x_send.at[n + 2], x_recv.at[n + 2], dev(*to)) for n, (s, d, to) in enumerate(moves)
-        ]
-        for h in sides:
-            h.start()
-        halos = halos + sides
+        for g in gathers + halos:
+            g.start()
         for g in gathers:
             g.wait_recv()
-    coarse[4] = c_recv[lax.rem(gy - blk[gy, gx] // 4 + GY, GY)]
+    coarse[4] = c_recv[lax.rem(gy - blk[gx, 0, gy] // 4 + GY, GY)]
     if REMOTE:
         for dy, dx in near:
             slot = (1 - dy) * 3 + (1 - dx)
-            spread.append(remote(coarse.at[4], coarse.at[slot], n_send.at[slot], n_recv.at[slot], dev(dy, dx)))
+            rows = (pl.ds(0, 8), pl.ds(0, 32), pl.ds(24, 8))[dy + 1]
+            spread.append(
+                remote(coarse.at[4, rows], coarse.at[slot, rows], n_send.at[slot], n_recv.at[slot], dev(dy, dx))
+            )
         for n in spread:
             n.start()
 
@@ -137,7 +147,7 @@
     for dy, dx in near + [(0, 0)]:
         ok = (gy + dy >= 0) & (gy + dy < GY) & (gx + dx >= 0) & (gx + dx < GX)
         flag = jnp.where(ok, 1.0, 0.0)
-        at = ice_ref[jnp.clip(gy + dy, 0, GY - 1), jnp.clip(gx + dx, 0, GX - 1)]
+        at = ice_ref[jnp.clip(gx + dx, 0, GX - 1), jnp.clip(gy + dy, 0, GY - 1)]
         inside[dy, dx] = flag
         iced[dy, dx] = flag * at.astype(F32)
 
@@ -173,6 +183,10 @@
     for h in halos:
         h.wait()
 
+    for ref in (h_west, h_east):
+        ref[pl.ds(HALO + 128, 128)] = pltpu.roll(ref[pl.ds(HALO, 128)], 64, 1)
+        ref[pl.ds(0, HALO)] = pltpu.roll(ref[pl.ds(0, HALO)], 64, 1)
+
     keep = [region(cls, inside) for cls in range(3)]
     for i in range(STRIP):
         at = pl.ds(i, 8, stride=STRIP)
@@ -180,32 +194,13 @@
         left = h_west[at, :]
         cls = 0 if i < 16 else (1 if i < 20 else 2)
         for f, dst in enumerate((T, FU, FV, OU, OV)):
-            r = pltpu.roll(right, 128 - 16 * f, 1) if f else right
-            l = pltpu.roll(left, 16 * f, 1) if f else left
+            r = pltpu.roll(right, 128 - shifts[f], 1) if f else right
+            l = pltpu.roll(left, shifts[f], 1) if f else left
             edge = jnp.where(lane < HALO, r, jnp.where(lane >= 128 - HALO, l, 0.0))
             x = jnp.stack([nat[f, 0, at, :], nat[f, 1, at, :], edge])
             if f == 0:
                 x = jnp.where(keep[cls] > 0.0, x, 0.0)
             dst[i] = x
-
-    for n in spread:
-        n.wait_recv()
-    for g, dx in enumerate((0, 1, -1)):
-        flat = jnp.concatenate(
-            [coarse[1 + dx, pl.ds(24, 8)], coarse[4 + dx], coarse[7 + dx, pl.ds(0, 8)]], axis=0
-        )
-        flat = jnp.exp(flat)
-        cext[g, pl.ds(0, 48, stride=2), :] = flat
-        cext[g, pl.ds(1, 48, stride=2), :] = pltpu.roll(flat, 64, 1)
-    quarter = lane // 4
-    for i in range(GROUP):
-        at = pl.ds(12 + i, 8, stride=GROUP)
-        mid, right, left = (cext[g, at, :] for g in range(3))
-        edges = jnp.where(lane < 64, right, pltpu.roll(left, 64, 1))
-        t0 = jnp.take_along_axis(mid, quarter, axis=1)
-        t1 = jnp.take_along_axis(mid, quarter + 32, axis=1)
-        t2 = jnp.take_along_axis(edges, jnp.where(lane < 64, quarter, 96 + quarter), axis=1)
-        FR[i] = jnp.stack([t0, t1, t2])
 
     base = float(visc_scale * np.power(strain_floor, -1.0 / 3.0))
 
@@ -300,6 +295,26 @@
     zero = (U0, UE0, UW0, V0, VE0, VW0)
     one = (U1, UE1, UW1, V1, VE1, VW1)
     viscosity(None)
+
+    for n in spread:
+        n.wait_recv()
+    for g, dx in enumerate((0, 1, -1)):
+        flat = jnp.concatenate(
+            [coarse[1 + dx, pl.ds(24, 8)], coarse[4 + dx], coarse[7 + dx, pl.ds(0, 8)]], axis=0
+        )
+        flat = jnp.exp(flat)
+        cext[g, pl.ds(0, 48, stride=2), :] = flat
+        cext[g, pl.ds(1, 48, stride=2), :] = pltpu.roll(flat, 64, 1)
+    quarter = lane // 4
+    for i in range(GROUP):
+        at = pl.ds(12 + i, 8, stride=GROUP)
+        mid, right, left = (cext[g, at, :] for g in range(3))
+        edges = jnp.where(lane < 64, right, pltpu.roll(left, 64, 1))
+        t0 = jnp.take_along_axis(mid, quarter, axis=1)
+        t1 = jnp.take_along_axis(mid, quarter + 32, axis=1)
+        t2 = jnp.take_along_axis(edges, jnp.where(lane < 64, quarter, 96 + quarter), axis=1)
+        FR[i] = jnp.stack([t0, t1, t2])
+
     sweep(None, one, FU, FV, True)
     sweep(one, zero, FU, FV, False)
 
@@ -364,33 +379,41 @@
     grad[...] = jnp.where(wide < 64, even, odd)
 
     first, second, third = [], [], []
+    for g in range(GX):
+        part[g] = grad[pl.ds(4 * g, 4), :]
     if REMOTE:
         first = [
-            remote(grad, tiles.at[off], a_send.at[off], a_recv.at[off], dev(off, 0)) for off in range(1, GY)
+            remote(part.at[lax.rem(gx + off, GX)], slots.at[off], b_send.at[off], b_recv.at[off], dev(0, off))
+            for off in range(1, GX)
         ]
     for c in first:
         c.start()
-    tiles[0] = grad[...]
+    slots[0] = part[gx]
+    owners = [blk[lax.rem(gx - off + GX, GX), 0, gy] for off in range(GX)]
+    which = lax.broadcasted_iota(jnp.int32, (16, 128), 0) % 4
     for c in first:
         c.wait_recv()
-    for k in range(4):
-        total = jnp.zeros((32, 128), F32)
-        for off in range(GY):
-            owner = blk[lax.rem(gy - off + GY, GY), gx]
-            total = total + jnp.where(owner == 4 * gy + k, tiles[off], 0.0)
-        for g in range(GX):
-            part[g, pl.ds(4 * k, 4)] = total[4 * g:4 * g + 4]
+    cells = []
+    for t in range(GX):
+        x = slots[t]
+        cells.append(jnp.concatenate([jnp.broadcast_to(x[j:j + 1], (4, 128)) for j in range(4)], axis=0))
     if REMOTE:
-        for off in range(1, GX):
-            to = lax.rem(gx + off, GX)
-            second.append(remote(part.at[to], slots.at[off], b_send.at[off], b_recv.at[off], dev(0, off)))
-    for c in second:
-        c.start()
-    for c in second:
-        c.wait_recv()
-    total = part[gx]
-    for off in range(1, GX):
-        total = total + slots[off]
+        second = [
+            remote(sums.at[off], tiles.at[off], a_send.at[off], a_recv.at[off], dev(off, 0)) for off in range(1, GY)
+        ]
+    for off in list(range(1, GY)) + [0]:
+        lowest = 4 * lax.rem(gy + off, GY)
+        total = jnp.zeros((16, 128), F32)
+        for t in range(GX):
+            total = total + jnp.where(which == owners[t] - lowest, cells[t], 0.0)
+        sums[off] = total
+        if off > 0 and REMOTE:
+            second[off - 1].start()
+    total = sums[0]
+    for off in range(1, GY):
+        if REMOTE:
+            second[off - 1].wait_recv()
+        total = total + tiles[off]
     red[...] = total
     if REMOTE:
         third = [
@@ -402,8 +425,8 @@
     for c in third:
         c.wait()
     for g in range(GX):
-        for k in range(4):
-            out_g[k, pl.ds(4 * g, 4)] = gathered[g, pl.ds(4 * k, 4)]
+        for j in range(4):
+            out_g[:, pl.ds((4 * g + j) * 128, 128)] = gathered[g, pl.ds(4 * j, 4)]
     for c in gathers + spread + first + second:
         c.wait_send()
     for s in stores:
@@ -413,7 +436,7 @@
 def call(*operands):
     shape = jax.ShapeDtypeStruct
     dma = pltpu.SemaphoreType.DMA
-    anywhere = pl.BlockSpec(memory_space=pl.ANY)
+    hbm = pl.BlockSpec(memory_space=pltpu.HBM)
     smem = pl.BlockSpec(memory_space=pltpu.SMEM)
     vmem = pl.BlockSpec(memory_space=pltpu.VMEM)
     field = pltpu.VMEM((STRIP, LT, 8, 128), F32)
@@ -422,15 +445,17 @@
     return pl.pallas_call(
         kernel,
         name="friction_gradient",
-        out_shape=(shape((TILE, TILE), F32), shape((TILE, TILE), F32), shape((4, 32, 128), F32)),
-        in_specs=[smem, smem, anywhere, anywhere, anywhere, vmem],
-        out_specs=[anywhere, anywhere, vmem],
+        out_shape=(shape((TILE, TILE), F32), shape((TILE, TILE), F32), shape((4, 4096), F32)),
+        in_specs=[smem, smem, hbm, hbm, hbm, hbm],
+        out_specs=[hbm, hbm, vmem],
         scratch_shapes=[
             pltpu.VMEM((5, 2, EXT, 128), F32),
-            pltpu.VMEM((TILE, 128), F32),
-            pltpu.VMEM((TILE, 128), F32),
+            pltpu.VMEM((128, 128), F32),
+            pltpu.VMEM((128, 128), F32),
             pltpu.VMEM((EXT, 128), F32),
             pltpu.VMEM((EXT, 128), F32),
+            pltpu.VMEM((4, 4096), F32),
+            pltpu.VMEM((4, 32, 128), F32),
             pltpu.VMEM((GY, 32, 128), F32),
             pltpu.VMEM((GY, 32, 128), F32),
             pltpu.VMEM((9, 32, 128), F32),
@@ -442,27 +467,27 @@
         ] + [padded] * 12 + [
             pltpu.VMEM((72, 128), F32),
             flat,
-            pltpu.VMEM((GY, 32, 128), F32),
-            pltpu.VMEM((GX, 16, 128), F32),
-            pltpu.VMEM((GX, 16, 128), F32),
+            pltpu.VMEM((GY, 16, 128), F32),
+            pltpu.VMEM((GY, 16, 128), F32),
+            pltpu.VMEM((GX, 4, 128), F32),
+            pltpu.VMEM((GX, 4, 128), F32),
             pltpu.VMEM((16, 128), F32),
             pltpu.VMEM((GX, 16, 128), F32),
-            dma((5, 2)), dma((2, 2)),
-            dma((GY,)), dma((GY,)), dma((8,)), dma((8,)), dma((9,)), dma((9,)),
+            dma, dma((5, 2)), dma((2, 2)),
+            dma((GY,)), dma((GY,)), dma((10,)), dma((10,)), dma((9,)), dma((9,)),
             dma((GY,)), dma((GY,)), dma((GX,)), dma((GX,)), dma((GX,)), dma((GX,)),
         ],
         compiler_params=pltpu.CompilerParams(
-            vmem_limit_bytes=48 << 20,
+            vmem_limit_bytes=60 << 20,
             **(dict(collective_id=0, has_side_effects=True) if REMOTE else {}),
         ),
     )(*operands)
 
 
 def per_device(thickness, driving, observed, control, ice_mask, tile_block):
-    vel_u, vel_v, total = call(
-        tile_block.reshape(GY, GX), ice_mask, thickness, driving, observed, control.reshape(4, 32, 128)
+    return call(
+        tile_block.transpose(1, 2, 0), ice_mask.T, thickness, driving, observed, control
     )
-    return vel_u, vel_v, total.reshape(4, 4096)
 
 
 def solution(mesh):

time: 61.2 us -> 51.5 us (0.84)
  Pallas kernels: 53.5 us -> 47.2 us
  local copies, waits for them, and re-layouts: 6.79 us -> 3.21 us
    pallas_call x1, Pallas kernels: 53.5 us -> 47.2 us  [call(): pl.pallas_call(kernel, name='friction_gradient', out_shape=(shape((TILE,...]
    unnamed x13 -> x7, local copies, waits for them, and re-layouts: 6.72 us -> 3.21 us
where the time goes in v3:
time: 51.5 us; the launch traced here: 51.1 us
  Pallas kernels  47.2 us (92%)
  local copies, waits for them, and re-layouts  3.21 us (6%)
  between operations  0.65 us (1%)
    pallas_call x1, Pallas kernels, call(): pl.pallas_call(kernel, name='friction_gradient', out_shape=(shape((TILE,...  47.2 us
    unnamed x7, local copies, waits for them, and re-layouts  3.21 us

profile of v3, /device:TPU:0, one launch (start us, length us, event | category | flops | bytes accessed | tf_op | source)
XLA Modules:
  0.0 51.1 jit_solution(7421871428384931764)
XLA Ops:
  0.6 47.2 %friction_gradient.1 = (f32[256,256]{1,0:T(8,128)}, f32[256,256]{1,0:T(8,128)}, f32[4,4096]{1,0:T(4,128)}) custom-call(s32[8,1,16]{2,1,0:T(1,128)} %bitcast.2, s32[8,16]{1,0:T(8,128)} %bitcast.3, f32[256,256]{1,0:T(8,128)} %thick.1, f32[2,256,256]{2,1,0:T(8,128)} %drv.1, f32[2,256,256]{2,1,0:T(8,128)} %obs.1, f32[4,4096]{1,0:T(4,128)} %ctl.1), custom_call_target="tpu_custom_call" | custom-call | tf_op jit(solution)/shard_map/friction_gradient/pallas_call | solution.py:445
  47.8 0.0 copy-start
  47.9 1.7 %copy.12 = f32[256,256]{1,0:T(8,128)} copy(f32[256,256]{1,0:T(8,128)} %get-tuple-element.6) | data formatting | bytes 524288
  49.6 0.0 copy-done
  49.6 0.0 copy-start.1
  49.6 0.7 %copy.13 = f32[256,256]{1,0:T(8,128)} copy(f32[256,256]{1,0:T(8,128)S(1)} %copy-done) | data formatting | bytes 524288
  50.3 0.2 copy-done.1
  50.4 0.6 %copy.14 = f32[4,4096]{1,0:T(4,128)} copy(f32[4,4096]{1,0:T(4,128)S(1)} %copy-done.1) | data formatting | bytes 131072
Async XLA Ops:
  47.8 1.7 %copy-start = (f32[256,256]{1,0:T(8,128)S(1)}, f32[256,256]{1,0:T(8,128)}, u32[]{:S(2)}) copy-start(f32[256,256]{1,0:T(8,128)} %get-tuple-element.7) | copy-start | bytes 786436
  49.6 0.9 %copy-start.1 = (f32[4,4096]{1,0:T(4,128)S(1)}, f32[4,4096]{1,0:T(4,128)}, u32[]{:S(2)}) copy-start(f32[4,4096]{1,0:T(4,128)} %get-tuple-element.8) | copy-start | bytes 196612

commit v4 on v3

--- a/solution.py
+++ b/solution.py
@@ -29,11 +29,11 @@
 def kernel(
     blk, ice_ref, thick, drv, obs, ctl,
     out_u, out_v, out_g,
-    nat, pack_w, pack_e, h_west, h_east, c_in, c_own, c_send, c_recv, coarse, cext,
+    nat, pack_w, pack_e, h_west, h_east, c_in, c_own, c_side, c_ends, c_send, c_recv, coarse, cext,
     T, FU, FV, OU, OV, FR, IC, H, A, B, IU, IV,
     U0, UE0, UW0, V0, VE0, VW0, U1, UE1, UW1, V1, VE1, VW1,
     small, grad, sums, tiles, part, slots, red, gathered,
-    k_sem, l_sem, o_sem, g_send, g_recv, x_send, x_recv, n_send, n_recv,
+    k_sem, l_sem, o_sem, g_send, g_recv, x_send, x_recv,
     a_send, a_recv, b_send, b_recv, d_send, d_recv,
 ):
     gx = lax.axis_index("gx")
@@ -47,6 +47,8 @@
             src_ref=src, dst_ref=dst, send_sem=ss, recv_sem=rs, device_id=to, device_id_type=MESH
         )
 
+    rates = pltpu.make_async_copy(ctl, c_in, k_sem)
+    rates.start()
     near = [(dy, dx) for dy in (-1, 0, 1) for dx in (-1, 0, 1) if (dy, dx) != (0, 0)]
     if REMOTE:
         barrier = pltpu.get_barrier_semaphore()
@@ -55,16 +57,13 @@
         for dy, dx in peers:
             pl.semaphore_signal(barrier, inc=1, device_id=dev(dy, dx), device_id_type=MESH)
 
-    rates = pltpu.make_async_copy(ctl, c_in, k_sem)
-    rates.start()
-
     inner = pl.ds(HALO, TILE)
     loads = []
-    for f, src in enumerate((thick, drv.at[0], drv.at[1], obs.at[0], obs.at[1])):
-        for c in range(2):
-            loads.append(
-                pltpu.make_async_copy(src.at[:, pl.ds(c * 128, 128)], nat.at[f, c, inner], l_sem.at[f, c])
-            )
+    for c in range(2):
+        cols = pl.ds(c * 128, 128)
+        loads.append(pltpu.make_async_copy(thick.at[:, cols], nat.at[0, c, inner], l_sem.at[0, c]))
+        loads.append(pltpu.make_async_copy(drv.at[:, :, cols], nat.at[pl.ds(1, 2), c, inner], l_sem.at[1, c]))
+        loads.append(pltpu.make_async_copy(obs.at[:, :, cols], nat.at[pl.ds(3, 2), c, inner], l_sem.at[2, c]))
     for copy in loads:
         copy.start()
 
@@ -77,14 +76,50 @@
         x = c_in[:, pl.ds(t * 128, 128)]
         for k in range(4):
             c_own[k, pl.ds(t, 1)] = x[k:k + 1]
+    for k in range(4):
+        for g in range(4):
+            x = c_own[k, pl.ds(8 * g, 8)]
+            right = pltpu.roll(x, 4 * g, 1) if g else x
+            left = pltpu.roll(x, 128 - 4 * g, 1) if g else x
+            if g == 0:
+                side = x
+            else:
+                side = jnp.where((lane % 64 >= 4 * g) & (lane % 64 < 32), right, side)
+                side = jnp.where((lane % 64 >= 32) & (lane % 64 < 64 - 4 * g), left, side)
+        c_side[k] = side
+        for half in range(2):
+            c_ends[k, pl.ds(4 * half, 2)] = c_own[k, pl.ds(30, 2)]
+            c_ends[k, pl.ds(4 * half + 2, 2)] = c_own[k, pl.ds(0, 2)]
+    eastern = lane % 64 < 32
+
+    seen = [
+        [blk[lax.rem(gx + dx + GX, GX), 0, lax.rem(gy + dy, GY)] for dy in range(GY)] for dx in (-1, 0, 1)
+    ]
+
+    def tile(dy, dx):
+        return seen[dx + 1][dy % GY]
+
     for off in range(GY):
-        c_send[off] = c_own[lax.rem(blk[gx, 0, lax.rem(gy + off, GY)], 4)]
+        pick = {
+            (dy, dx): tile(off + dy, dx) & 3 for dy in (-1, 0, 1) for dx in (-1, 0, 1)
+        }
+        c_send[off, pl.ds(0, 32)] = c_own[pick[0, 0]]
+        c_send[off, pl.ds(32, 8)] = jnp.where(eastern, c_side[pick[0, 1]], c_side[pick[0, -1]])
+        corner_n = jnp.where(eastern, c_ends[pick[-1, 1]], c_ends[pick[-1, -1]])
+        corner_s = jnp.where(eastern, c_ends[pick[1, 1]], c_ends[pick[1, -1]])
+        ends = jnp.where(sub < 2, c_ends[pick[-1, 0]], c_ends[pick[1, 0]])
+        c_send[off, pl.ds(40, 8)] = jnp.where(sub < 4, ends, jnp.where(sub < 6, corner_n, corner_s))
+    gathers = []
+    if REMOTE:
+        pl.semaphore_wait(barrier, len(peers))
+        gathers = [
+            remote(c_send.at[off], c_recv.at[off], g_send.at[off], g_recv.at[off], dev(off, 0))
+            for off in range(1, GY)
+        ]
+        for g in gathers:
+            g.start()
     c_recv[0] = c_send[0]
 
-    for f in (3, 4):
-        for c in range(2):
-            nat[f, c, pl.ds(0, 8)] = jnp.zeros((8, 128), F32)
-            nat[f, c, pl.ds(EXT - 8, 8)] = jnp.zeros((8, 128), F32)
     for copy in loads:
         copy.wait()
     shifts = (0, 16, 32, 48, 56)
@@ -104,44 +139,24 @@
         pack_w[pl.ds(t * 8, 8), :] = w
         pack_e[pl.ds(t * 8, 8), :] = e
 
-    gathers, halos, spread = [], [], []
+    halos = []
     if REMOTE:
-        pl.semaphore_wait(barrier, len(peers))
-        gathers = [
-            remote(c_send.at[off], c_recv.at[off], g_send.at[off], g_recv.at[off], dev(off, 0))
-            for off in range(1, GY)
-        ]
-        main, obs2 = pl.ds(0, 3), pl.ds(3, 2)
         half = pl.ds(HALO, 128)
         head, tail = pl.ds(0, HALO), pl.ds(112, HALO)
         first, last = pl.ds(0, HALO), pl.ds(TILE + HALO, HALO)
         moves = [
             (pack_e, h_west.at[half], (0, 1)),
             (pack_w, h_east.at[half], (0, -1)),
-            (nat.at[main, :, pl.ds(TILE, HALO)], nat.at[main, :, first], (1, 0)),
-            (nat.at[main, :, pl.ds(HALO, HALO)], nat.at[main, :, last], (-1, 0)),
+            (nat.at[:, :, pl.ds(TILE, HALO)], nat.at[:, :, first], (1, 0)),
+            (nat.at[:, :, pl.ds(HALO, HALO)], nat.at[:, :, last], (-1, 0)),
             (pack_e.at[tail], h_west.at[first], (1, 1)),
             (pack_e.at[head], h_west.at[last], (-1, 1)),
             (pack_w.at[tail], h_east.at[first], (1, -1)),
             (pack_w.at[head], h_east.at[last], (-1, -1)),
-            (nat.at[obs2, :, pl.ds(TILE + 8, 8)], nat.at[obs2, :, pl.ds(8, 8)], (1, 0)),
-            (nat.at[obs2, :, pl.ds(HALO, 8)], nat.at[obs2, :, pl.ds(TILE + HALO, 8)], (-1, 0)),
         ]
         halos = [remote(s, d, x_send.at[n], x_recv.at[n], dev(*to)) for n, (s, d, to) in enumerate(moves)]
-        for g in gathers + halos:
-            g.start()
-        for g in gathers:
-            g.wait_recv()
-    coarse[4] = c_recv[lax.rem(gy - blk[gx, 0, gy] // 4 + GY, GY)]
-    if REMOTE:
-        for dy, dx in near:
-            slot = (1 - dy) * 3 + (1 - dx)
-            rows = (pl.ds(0, 8), pl.ds(0, 32), pl.ds(24, 8))[dy + 1]
-            spread.append(
-                remote(coarse.at[4, rows], coarse.at[slot, rows], n_send.at[slot], n_recv.at[slot], dev(dy, dx))
-            )
-        for n in spread:
-            n.start()
+        for h in halos:
+            h.start()
 
     inside, iced = {}, {}
     for dy, dx in near + [(0, 0)]:
@@ -296,18 +311,30 @@
     one = (U1, UE1, UW1, V1, VE1, VW1)
     viscosity(None)
 
-    for n in spread:
-        n.wait_recv()
+    for g in gathers:
+        g.wait_recv()
+
+    def heard(dy, dx):
+        return lax.rem(gy - tile(dy, dx) // 4 + GY, GY)
+
+    both = jnp.where(eastern, c_recv[heard(0, 1), pl.ds(32, 8)], c_recv[heard(0, -1), pl.ds(32, 8)])
     for g, dx in enumerate((0, 1, -1)):
-        flat = jnp.concatenate(
-            [coarse[1 + dx, pl.ds(24, 8)], coarse[4 + dx], coarse[7 + dx, pl.ds(0, 8)]], axis=0
-        )
-        flat = jnp.exp(flat)
-        cext[g, pl.ds(0, 48, stride=2), :] = flat
-        cext[g, pl.ds(1, 48, stride=2), :] = pltpu.roll(flat, 64, 1)
+        row = 0 if dx == 0 else 4
+        coarse[g, pl.ds(0, 2)] = c_recv[heard(-1, dx), pl.ds(40, 8)][row:row + 2]
+        coarse[g, pl.ds(34, 2)] = c_recv[heard(1, dx), pl.ds(40, 8)][row + 2:row + 4]
+        coarse[g, pl.ds(36, 4)] = jnp.zeros((4, 128), F32)
+        if dx == 0:
+            coarse[g, pl.ds(2, 32)] = c_recv[heard(0, 0), pl.ds(0, 32)]
+        else:
+            for q in range(4):
+                shift = (128 - 4 * q if dx == 1 else 4 * q) % 128
+                coarse[g, pl.ds(2 + 8 * q, 8)] = pltpu.roll(both, shift, 1) if shift else both
+        flat = jnp.exp(coarse[g])
+        cext[g, pl.ds(0, 40, stride=2), :] = flat
+        cext[g, pl.ds(1, 40, stride=2), :] = pltpu.roll(flat, 64, 1)
     quarter = lane // 4
     for i in range(GROUP):
-        at = pl.ds(12 + i, 8, stride=GROUP)
+        at = pl.ds(i, 8, stride=GROUP)
         mid, right, left = (cext[g, at, :] for g in range(3))
         edges = jnp.where(lane < 64, right, pltpu.roll(left, 64, 1))
         t0 = jnp.take_along_axis(mid, quarter, axis=1)
@@ -427,7 +454,7 @@
     for g in range(GX):
         for j in range(4):
             out_g[:, pl.ds((4 * g + j) * 128, 128)] = gathered[g, pl.ds(4 * j, 4)]
-    for c in gathers + spread + first + second:
+    for c in gathers + first + second:
         c.wait_send()
     for s in stores:
         s.wait()
@@ -456,10 +483,12 @@
             pltpu.VMEM((EXT, 128), F32),
             pltpu.VMEM((4, 4096), F32),
             pltpu.VMEM((4, 32, 128), F32),
-            pltpu.VMEM((GY, 32, 128), F32),
-            pltpu.VMEM((GY, 32, 128), F32),
-            pltpu.VMEM((9, 32, 128), F32),
-            pltpu.VMEM((3, 96, 128), F32),
+            pltpu.VMEM((4, 8, 128), F32),
+            pltpu.VMEM((4, 8, 128), F32),
+            pltpu.VMEM((GY, 48, 128), F32),
+            pltpu.VMEM((GY, 48, 128), F32),
+            pltpu.VMEM((3, 40, 128), F32),
+            pltpu.VMEM((3, 80, 128), F32),
             field, field, field, field, field,
             pltpu.VMEM((GROUP, LT, 8, 128), F32),
             pltpu.VMEM((3, LT, 8, 128), F32),
@@ -473,8 +502,8 @@
             pltpu.VMEM((GX, 4, 128), F32),
             pltpu.VMEM((16, 128), F32),
             pltpu.VMEM((GX, 16, 128), F32),
-            dma, dma((5, 2)), dma((2, 2)),
-            dma((GY,)), dma((GY,)), dma((10,)), dma((10,)), dma((9,)), dma((9,)),
+            dma, dma((3, 2)), dma((2, 2)),
+            dma((GY,)), dma((GY,)), dma((8,)), dma((8,)),
             dma((GY,)), dma((GY,)), dma((GX,)), dma((GX,)), dma((GX,)), dma((GX,)),
         ],
         compiler_params=pltpu.CompilerParams(

time: 51.5 us -> 50 us (0.971)
  Pallas kernels: 47.2 us -> 45.9 us
    pallas_call x1, Pallas kernels: 47.2 us -> 45.9 us  [call(): pl.pallas_call(kernel, name='friction_gradient', out_shape=(shape((TILE,...]
where the time goes in v4:
time: 50 us; the launch traced here: 49.7 us
  Pallas kernels  45.9 us (92%)
  local copies, waits for them, and re-layouts  3.21 us (6%)
  between operations  0.65 us (1%)
    pallas_call x1, Pallas kernels, call(): pl.pallas_call(kernel, name='friction_gradient', out_shape=(shape((TILE,...  45.9 us
    unnamed x7, local copies, waits for them, and re-layouts  3.21 us

profile of v4, /device:TPU:0, one launch (start us, length us, event | category | flops | bytes accessed | tf_op | source)
XLA Modules:
  0.0 49.7 jit_solution(5779665509816923904)
XLA Ops:
  0.6 45.9 %friction_gradient.1 = (f32[256,256]{1,0:T(8,128)}, f32[256,256]{1,0:T(8,128)}, f32[4,4096]{1,0:T(4,128)}) custom-call(s32[8,1,16]{2,1,0:T(1,128)} %bitcast.2, s32[8,16]{1,0:T(8,128)} %bitcast.3, f32[256,256]{1,0:T(8,128)} %thick.1, f32[2,256,256]{2,1,0:T(8,128)} %drv.1, f32[2,256,256]{2,1,0:T(8,128)} %obs.1, f32[4,4096]{1,0:T(4,128)} %ctl.1), custom_call_target="tpu_custom_call" | custom-call | tf_op jit(solution)/shard_map/friction_gradient/pallas_call | solution.py:472
  46.5 0.0 copy-start
  46.5 1.7 %copy.12 = f32[256,256]{1,0:T(8,128)} copy(f32[256,256]{1,0:T(8,128)} %get-tuple-element.6) | data formatting | bytes 524288
  48.2 0.0 copy-done
  48.2 0.0 copy-start.1
  48.2 0.7 %copy.13 = f32[256,256]{1,0:T(8,128)} copy(f32[256,256]{1,0:T(8,128)S(1)} %copy-done) | data formatting | bytes 524288
  48.9 0.2 copy-done.1
  49.1 0.6 %copy.14 = f32[4,4096]{1,0:T(4,128)} copy(f32[4,4096]{1,0:T(4,128)S(1)} %copy-done.1) | data formatting | bytes 131072
Async XLA Ops:
  46.5 1.7 %copy-start = (f32[256,256]{1,0:T(8,128)S(1)}, f32[256,256]{1,0:T(8,128)}, u32[]{:S(2)}) copy-start(f32[256,256]{1,0:T(8,128)} %get-tuple-element.7) | copy-start | bytes 786436
  48.2 0.9 %copy-start.1 = (f32[4,4096]{1,0:T(4,128)S(1)}, f32[4,4096]{1,0:T(4,128)}, u32[]{:S(2)}) copy-start(f32[4,4096]{1,0:T(4,128)} %get-tuple-element.8) | copy-start | bytes 196612

commit v5 on v4

--- a/solution.py
+++ b/solution.py
@@ -11,13 +11,11 @@
 EXT = TILE + 2 * HALO
 STRIP = EXT // 8
 GROUP = STRIP // 4
-LT = 3
 PIC = 4
 ADJ = 6
 GX = 8
 GY = 16
-ROWS = 36
-MROWS = 36
+ROWS = 3
 REMOTE = True
 MESH = pl.DeviceIdType.MESH
 F32 = jnp.float32
@@ -69,7 +67,6 @@
 
     lane = lax.broadcasted_iota(jnp.int32, (8, 128), 1)
     sub = lax.broadcasted_iota(jnp.int32, (8, 128), 0)
-    lane3 = lax.broadcasted_iota(jnp.int32, (LT, 8, 128), 2)
 
     rates.wait()
     for t in range(32):
@@ -166,34 +163,78 @@
         inside[dy, dx] = flag
         iced[dy, dx] = flag * at.astype(F32)
 
-    def region(cls, table):
+    def m(i, c):
+        return 2 * (i + 1) + c
+
+    def p(i):
+        return 2 * (STRIP + 2) + 1 + i
+
+    within = lane % 32
+    block = lane // 32
+
+    def region(i, table):
+        base = jnp.full((8, 128), table[0, 0], F32)
+        if i < HALO:
+            return jnp.where(sub == 0, table[-1, 0], base)
+        if i >= TILE + HALO - 7 * STRIP:
+            return jnp.where(sub == 7, table[1, 0], base)
+        return base
+
+    def side_region(i, table):
+        row = sub * STRIP + block * GROUP + i
+
         def by_row(dx):
-            mid = jnp.full((8, 128), table[0, dx], F32)
-            if cls == 0:
-                return jnp.where(sub == 0, table[-1, dx], mid)
-            if cls == 2:
-                return jnp.where(sub == 7, table[1, dx], mid)
-            return mid
-
-        center = by_row(0)
-        edge = jnp.where(lane < HALO, by_row(1), jnp.where(lane >= 128 - HALO, by_row(-1), 0.0))
-        return jnp.stack([center, center, edge])
-
-    for cls in range(3):
-        IC[cls] = region(cls, iced)
-
-    def west(x):
-        y = pltpu.roll(x, 1, 2)
-        return jnp.where(lane3 == 0, jnp.concatenate([y[2:], y[:2]], axis=0), y)
-
-    def east(x):
-        y = pltpu.roll(x, 127, 2)
-        return jnp.where(lane3 == 127, jnp.concatenate([y[1:], y[:1]], axis=0), y)
+            return jnp.where(
+                row < HALO, table[-1, dx], jnp.where(row < HALO + TILE, table[0, dx], table[1, dx])
+            )
+
+        return jnp.where(within < HALO, by_row(1), by_row(-1))
+
+    def shifts_of(t0, t1, x):
+        w0 = [pltpu.roll(t, 1, 1) for t in t0]
+        w1 = [pltpu.roll(t, 1, 1) for t in t1]
+        e0 = [pltpu.roll(t, 127, 1) for t in t0]
+        e1 = [pltpu.roll(t, 127, 1) for t in t1]
+        wx = pltpu.roll(x, 1, 1)
+        ex = pltpu.roll(x, 127, 1)
+        west = [[], []]
+        east = [[], []]
+        west_x, east_x = wx, ex
+        for g in range(4):
+            from_x = wx if g == 3 else pltpu.roll(x, 97 - 32 * g, 1)
+            west[0].append(jnp.where(lane == 0, from_x, w0[g]))
+            west[1].append(jnp.where(lane == 0, w0[g], w1[g]))
+            edge = w1[g] if g == 0 else pltpu.roll(t1[g], 32 * g + 1, 1)
+            west_x = jnp.where(lane == 32 * g, edge, west_x)
+            from_x = ex if g == 0 else pltpu.roll(x, 127 - 32 * g, 1)
+            east[0].append(jnp.where(lane == 127, e1[g], e0[g]))
+            east[1].append(jnp.where(lane == 127, from_x, e1[g]))
+            edge = e0[g] if g == 3 else pltpu.roll(t0[g], 32 * g + 31, 1)
+            east_x = jnp.where(lane == 32 * g + 31, edge, east_x)
+        return east, east_x, west, west_x
+
+    def keep_all(ref, i, t, x):
+        for g in range(4):
+            for c in range(2):
+                ref[m(GROUP * g + i, c)] = t[c][g]
+        ref[p(i)] = x
+
+    def put(dst, i, u, ux, v, vx):
+        for refs, t, x in ((dst[:3], u, ux), (dst[3:], v, vx)):
+            east, east_x, west, west_x = shifts_of(t[0], t[1], x)
+            keep_all(refs[0], i, t, x)
+            keep_all(refs[1], i, east, east_x)
+            keep_all(refs[2], i, west, west_x)
 
     def wrap(refs):
         for ref in refs:
-            ref[0] = pltpu.roll(ref[STRIP], 1, 1)
-            ref[STRIP + 1] = pltpu.roll(ref[1], 7, 1)
+            for c in range(2):
+                ref[m(-1, c)] = pltpu.roll(ref[m(STRIP - 1, c)], 1, 0)
+                ref[m(STRIP, c)] = pltpu.roll(ref[m(0, c)], 7, 0)
+            y = pltpu.roll(ref[p(GROUP - 1)], 32, 1)
+            ref[p(-1)] = jnp.where(lane < 32, pltpu.roll(y, 1, 0), y)
+            y = pltpu.roll(ref[p(0)], 96, 1)
+            ref[p(GROUP)] = jnp.where(lane >= 96, pltpu.roll(y, 7, 0), y)
 
     for h in halos:
         h.wait()
@@ -202,73 +243,83 @@
         ref[pl.ds(HALO + 128, 128)] = pltpu.roll(ref[pl.ds(HALO, 128)], 64, 1)
         ref[pl.ds(0, HALO)] = pltpu.roll(ref[pl.ds(0, HALO)], 64, 1)
 
-    keep = [region(cls, inside) for cls in range(3)]
+    fields = (T, FU, FV, OU, OV)
     for i in range(STRIP):
         at = pl.ds(i, 8, stride=STRIP)
-        right = h_east[at, :]
-        left = h_west[at, :]
-        cls = 0 if i < 16 else (1 if i < 20 else 2)
-        for f, dst in enumerate((T, FU, FV, OU, OV)):
-            r = pltpu.roll(right, 128 - shifts[f], 1) if f else right
-            l = pltpu.roll(left, shifts[f], 1) if f else left
-            edge = jnp.where(lane < HALO, r, jnp.where(lane >= 128 - HALO, l, 0.0))
-            x = jnp.stack([nat[f, 0, at, :], nat[f, 1, at, :], edge])
+        for c in range(2):
+            for f, dst in enumerate(fields):
+                dst[m(i, c)] = nat[f, c, at, :]
+    for i in range(GROUP):
+        right = [h_east[pl.ds(GROUP * g + i, 8, stride=STRIP), :] for g in range(4)]
+        left = [h_west[pl.ds(GROUP * g + i, 8, stride=STRIP), :] for g in range(4)]
+        for f, dst in enumerate(fields):
+            x = None
+            for g in range(4):
+                r = (32 * g - shifts[f]) % 128
+                l = (32 * g + HALO - 112 + shifts[f]) % 128
+                r = pltpu.roll(right[g], r, 1) if r else right[g]
+                l = pltpu.roll(left[g], l, 1) if l else left[g]
+                y = jnp.where(within < HALO, r, l)
+                x = y if x is None else jnp.where(block == g, y, x)
             if f == 0:
-                x = jnp.where(keep[cls] > 0.0, x, 0.0)
-            dst[i] = x
+                x = jnp.where(side_region(i, inside) > 0.0, x, 0.0)
+            dst[p(i)] = x
+    for i in list(range(HALO)) + list(range(TILE + HALO - 7 * STRIP, STRIP)):
+        keep = region(i, inside) > 0.0
+        for c in range(2):
+            T[m(i, c)] = jnp.where(keep, T[m(i, c)], 0.0)
 
     base = float(visc_scale * np.power(strain_floor, -1.0 / 3.0))
-
-    def put(dst, i, u, v):
-        U, UE, UW, V, VE, VW = dst
-        U[i + 1] = u
-        UE[i + 1] = east(u)
-        UW[i + 1] = west(u)
-        V[i + 1] = v
-        VE[i + 1] = east(v)
-        VW[i + 1] = west(v)
+    every = [[m(GROUP * g + i, c) for c in range(2) for g in range(4)] + [p(i)] for i in range(GROUP)]
+
+    def step_of(at, by):
+        return at + 2 * by if at < p(-1) else at + by
+
+    def split(values):
+        return [values[:4], values[4:8]], values[8]
 
     def viscosity(src):
-        @pl.loop(0, STRIP // MROWS)
-        def _(it):
-            for k in range(MROWS):
-                i = it * MROWS + k
+        for spot, i in enumerate([0, GROUP - 1] + list(range(1, GROUP - 1))):
+            values = []
+            for at in every[i]:
                 if src is None:
-                    m = (0.5 * base) * T[i]
-                else:
-                    U, UE, UW, V, VE, VW = src
-                    ux = 0.5 * (UE[i + 1] - UW[i + 1])
-                    vx = 0.5 * (VE[i + 1] - VW[i + 1])
-                    uy = 0.5 * (U[i + 2] - U[i])
-                    vy = 0.5 * (V[i + 2] - V[i])
-                    sh = uy + vx
-                    strain = ux * ux + vy * vy + ux * vy + 0.25 * (sh * sh) + strain_floor
-                    m = (0.5 * visc_scale) * T[i] * jnp.exp2(jnp.log2(strain) * (-1.0 / 3.0))
-                H[i + 1] = m
-                A[i] = east(m)
-                B[i] = west(m)
-
-        wrap([H])
+                    values.append((0.5 * base) * T[at])
+                    continue
+                U, UE, UW, V, VE, VW = src
+                ux = 0.5 * (UE[at] - UW[at])
+                vx = 0.5 * (VE[at] - VW[at])
+                uy = 0.5 * (U[step_of(at, 1)] - U[step_of(at, -1)])
+                vy = 0.5 * (V[step_of(at, 1)] - V[step_of(at, -1)])
+                sh = uy + vx
+                strain = ux * ux + vy * vy + ux * vy + 0.25 * (sh * sh) + strain_floor
+                values.append((0.5 * visc_scale) * T[at] * jnp.exp2(jnp.log2(strain) * (-1.0 / 3.0)))
+            t, x = split(values)
+            east, east_x, west, west_x = shifts_of(t[0], t[1], x)
+            keep_all(H, i, t, x)
+            keep_all(A, i, east, east_x)
+            keep_all(B, i, west, west_x)
+            if spot == 1:
+                wrap([H])
 
     def sweep(src, dst, fu_ref, fv_ref, fresh):
-        @pl.loop(0, STRIP // ROWS)
-        def _(it):
-            b = it * ROWS
-            new_u = [[None] * LT for _ in range(ROWS)]
-            new_v = [[None] * LT for _ in range(ROWS)]
+        starts = list(range(0, GROUP, ROWS))
+        for spot, s in enumerate([starts[0], starts[-1]] + starts[1:-1]):
+            new_u = [[None] * 9 for _ in range(ROWS)]
+            new_v = [[None] * 9 for _ in range(ROWS)]
             n = ROWS + 2
-            for c in range(LT):
-                h = [H[b + j, c] for j in range(n)]
+            for lot in range(9):
+                spots = [step_of(every[s][lot], j - 1) for j in range(n)]
+                h = [H[at] for at in spots]
                 face = [h[j] + h[j + 1] for j in range(n - 1)]
                 if src is not None:
-                    u, ue, uw, v, ve, vw = ([ref[b + j, c] for j in range(n)] for ref in src)
+                    u, ue, uw, v, ve, vw = ([ref[at] for at in spots] for ref in src)
                     q = [h[j] * (ve[j] - vw[j]) for j in range(n)]
                     r = [h[j] * (ue[j] - uw[j]) for j in range(n)]
                 for k in range(ROWS):
                     j = k + 1
-                    i = b + k
-                    a = A[i, c]
-                    w_ = B[i, c]
+                    at = spots[j]
+                    a = A[at]
+                    w_ = B[at]
                     fe = h[j] + a
                     fw = h[j] + w_
                     so = face[j]
@@ -276,21 +327,23 @@
                     if fresh:
                         ew = fe + fw
                         sn = so + no
-                        fr = FR[it * (ROWS // 4) + k // 4, c]
-                        step = i // 4
-                        cls = jnp.where(step < 4, 0, jnp.where(step < 5, 1, 2))
-                        ice = IC[cls, c]
-                        if c == 2:
-                            fr = jnp.where(ice > 0.0, fr, 1.0)
+                        step = s + k
+                        if lot < 8:
+                            step = GROUP * (lot % 4) + step
+                            fr = FR[2 * (step // 4) + lot // 4]
+                            ice = region(step, iced)
+                        else:
+                            fr = FR[2 * GROUP + step]
+                            ice = IC[step]
                         iu = ice / (fr + 4.0 * ew + sn)
                         iv = ice / (fr + ew + 4.0 * sn)
-                        IU[i, c] = iu
-                        IV[i, c] = iv
+                        IU[at] = iu
+                        IV[at] = iv
                     else:
-                        iu = IU[i, c]
-                        iv = IV[i, c]
-                    fu = fu_ref[i, c]
-                    fv = fv_ref[i, c]
+                        iu = IU[at]
+                        iv = IV[at]
+                    fu = fu_ref[at]
+                    fv = fv_ref[at]
                     if src is not None:
                         cu = a * (ve[j + 1] - ve[j - 1]) - w_ * (vw[j + 1] - vw[j - 1]) + 0.5 * (q[j + 1] - q[j - 1])
                         cv = 0.5 * (a * (ue[j + 1] - ue[j - 1]) - w_ * (uw[j + 1] - uw[j - 1])) + (r[j + 1] - r[j - 1])
@@ -300,12 +353,12 @@
                         sv = so * v[j + 1] + no * v[j - 1]
                         fu = fu + 4.0 * tu + su + cu
                         fv = fv + tv + 4.0 * sv + cv
-                    new_u[k][c] = iu * fu
-                    new_v[k][c] = iv * fv
+                    new_u[k][lot] = iu * fu
+                    new_v[k][lot] = iv * fv
             for k in range(ROWS):
-                put(dst, b + k, jnp.stack(new_u[k]), jnp.stack(new_v[k]))
-
-        wrap(dst)
+                put(dst, s + k, *split(new_u[k]), *split(new_v[k]))
+            if spot == 1:
+                wrap(dst)
 
     zero = (U0, UE0, UW0, V0, VE0, VW0)
     one = (U1, UE1, UW1, V1, VE1, VW1)
@@ -333,14 +386,22 @@
         cext[g, pl.ds(0, 40, stride=2), :] = flat
         cext[g, pl.ds(1, 40, stride=2), :] = pltpu.roll(flat, 64, 1)
     quarter = lane // 4
+    sides = []
     for i in range(GROUP):
         at = pl.ds(i, 8, stride=GROUP)
         mid, right, left = (cext[g, at, :] for g in range(3))
         edges = jnp.where(lane < 64, right, pltpu.roll(left, 64, 1))
-        t0 = jnp.take_along_axis(mid, quarter, axis=1)
-        t1 = jnp.take_along_axis(mid, quarter + 32, axis=1)
-        t2 = jnp.take_along_axis(edges, jnp.where(lane < 64, quarter, 96 + quarter), axis=1)
-        FR[i] = jnp.stack([t0, t1, t2])
+        FR[2 * i] = jnp.take_along_axis(mid, quarter, axis=1)
+        FR[2 * i + 1] = jnp.take_along_axis(mid, quarter + 32, axis=1)
+        sides.append(
+            jnp.take_along_axis(edges, jnp.where(within < HALO, within // 4, 120 + within // 4), axis=1)
+        )
+    for i in range(GROUP):
+        x = sides[i // 4]
+        for g in range(1, 4):
+            x = jnp.where(block == g, sides[(GROUP * g + i) // 4], x)
+        FR[2 * GROUP + i] = x
+        IC[i] = side_region(i, iced)
 
     sweep(None, one, FU, FV, True)
     sweep(one, zero, FU, FV, False)
@@ -351,23 +412,25 @@
         sweep(zero, one, FU, FV, True)
         sweep(one, zero, FU, FV, False)
 
-    @pl.loop(0, STRIP // 4)
-    def _(it):
-        for k in range(4):
-            i = it * 4 + k
-            u = U0[i + 1]
-            v = V0[i + 1]
-            FU[i] = u
-            FV[i] = v
-            at = pl.ds(i, 8, stride=STRIP)
-            for c in range(2):
-                nat[0, c, at, :] = u[c]
-                nat[1, c, at, :] = v[c]
-            mu = u - OU[i]
-            mv = v - OV[i]
-            OU[i] = mu
-            OV[i] = mv
-            put(one, i, IU[i] * mu, IV[i] * mv)
+    for i in range(GROUP):
+        new_u, new_v = [], []
+        for at in every[i]:
+            u = U0[at]
+            v = V0[at]
+            FU[at] = u
+            FV[at] = v
+            mu = u - OU[at]
+            mv = v - OV[at]
+            OU[at] = mu
+            OV[at] = mv
+            new_u.append(IU[at] * mu)
+            new_v.append(IV[at] * mv)
+        put(one, i, *split(new_u), *split(new_v))
+    for i in range(STRIP):
+        at = pl.ds(i, 8, stride=STRIP)
+        for c in range(2):
+            nat[0, c, at, :] = FU[m(i, c)]
+            nat[1, c, at, :] = FV[m(i, c)]
 
     stores = []
     for f, dst in enumerate((out_u, out_v)):
@@ -390,11 +453,11 @@
         total = None
         for k in range(4):
             j = i * 4 + k
-            cell = [FU[j, c] * U0[j + 1, c] + FV[j, c] * V0[j + 1, c] for c in range(2)]
+            cell = [FU[m(j, c)] * U0[m(j, c)] + FV[m(j, c)] * V0[m(j, c)] for c in range(2)]
             total = cell if total is None else [total[c] + cell[c] for c in range(2)]
         spots = []
         for c in range(2):
-            x = -FR[i, c] * total[c]
+            x = -FR[2 * i + c] * total[c]
             x = x + pltpu.roll(x, 127, 1)
             x = x + pltpu.roll(x, 126, 1)
             spots.append(jnp.take_along_axis(x, (lane % 32) * 4, axis=1))
@@ -466,8 +529,7 @@
     hbm = pl.BlockSpec(memory_space=pltpu.HBM)
     smem = pl.BlockSpec(memory_space=pltpu.SMEM)
     vmem = pl.BlockSpec(memory_space=pltpu.VMEM)
-    field = pltpu.VMEM((STRIP, LT, 8, 128), F32)
-    padded = pltpu.VMEM((STRIP + 2, LT, 8, 128), F32)
+    field = pltpu.VMEM((2 * (STRIP + 2) + GROUP + 2, 8, 128), F32)
     flat = pltpu.VMEM((32, 128), F32)
     return pl.pallas_call(
         kernel,
@@ -490,10 +552,10 @@
             pltpu.VMEM((3, 40, 128), F32),
             pltpu.VMEM((3, 80, 128), F32),
             field, field, field, field, field,
-            pltpu.VMEM((GROUP, LT, 8, 128), F32),
-            pltpu.VMEM((3, LT, 8, 128), F32),
-            padded, field, field, field, field,
-        ] + [padded] * 12 + [
+            pltpu.VMEM((3 * GROUP, 8, 128), F32),
+            pltpu.VMEM((GROUP, 8, 128), F32),
+            field, field, field, field, field,
+        ] + [field] * 12 + [
             pltpu.VMEM((72, 128), F32),
             flat,
             pltpu.VMEM((GY, 16, 128), F32),

time: 50 us -> 48.7 us (0.974)
  Pallas kernels: 45.9 us -> 44.6 us
    pallas_call x1, Pallas kernels: 45.9 us -> 44.6 us  [call(): pl.pallas_call(kernel, name='friction_gradient', out_shape=(shape((TILE,...]
where the time goes in v5:
time: 48.7 us; the launch traced here: 48.4 us
  Pallas kernels  44.6 us (92%)
  local copies, waits for them, and re-layouts  3.21 us (7%)
  between operations  0.65 us (1%)
    pallas_call x1, Pallas kernels, call(): pl.pallas_call(kernel, name='friction_gradient', out_shape=(shape((TILE,...  44.6 us
    unnamed x7, local copies, waits for them, and re-layouts  3.21 us

profile of v5, /device:TPU:0, one launch (start us, length us, event | category | flops | bytes accessed | tf_op | source)
XLA Modules:
  0.0 48.4 jit_solution(10021017900479173661)
XLA Ops:
  0.6 44.6 %friction_gradient.1 = (f32[256,256]{1,0:T(8,128)}, f32[256,256]{1,0:T(8,128)}, f32[4,4096]{1,0:T(4,128)}) custom-call(s32[8,1,16]{2,1,0:T(1,128)} %bitcast.2, s32[8,16]{1,0:T(8,128)} %bitcast.3, f32[256,256]{1,0:T(8,128)} %thick.1, f32[2,256,256]{2,1,0:T(8,128)} %drv.1, f32[2,256,256]{2,1,0:T(8,128)} %obs.1, f32[4,4096]{1,0:T(4,128)} %ctl.1), custom_call_target="tpu_custom_call" | custom-call | tf_op jit(solution)/shard_map/friction_gradient/pallas_call | solution.py:534
  45.2 0.0 copy-start
  45.2 1.7 %copy.12 = f32[256,256]{1,0:T(8,128)} copy(f32[256,256]{1,0:T(8,128)} %get-tuple-element.6) | data formatting | bytes 524288
  46.9 0.0 copy-done
  46.9 0.0 copy-start.1
  46.9 0.7 %copy.13 = f32[256,256]{1,0:T(8,128)} copy(f32[256,256]{1,0:T(8,128)S(1)} %copy-done) | data formatting | bytes 524288
  47.6 0.2 copy-done.1
  47.8 0.6 %copy.14 = f32[4,4096]{1,0:T(4,128)} copy(f32[4,4096]{1,0:T(4,128)S(1)} %copy-done.1) | data formatting | bytes 131072
Async XLA Ops:
  45.2 1.7 %copy-start = (f32[256,256]{1,0:T(8,128)S(1)}, f32[256,256]{1,0:T(8,128)}, u32[]{:S(2)}) copy-start(f32[256,256]{1,0:T(8,128)} %get-tuple-element.7) | copy-start | bytes 786436
  46.9 0.9 %copy-start.1 = (f32[4,4096]{1,0:T(4,128)S(1)}, f32[4,4096]{1,0:T(4,128)}, u32[]{:S(2)}) copy-start(f32[4,4096]{1,0:T(4,128)} %get-tuple-element.8) | copy-start | bytes 196612

commit v6 on v5

--- a/solution.py
+++ b/solution.py
@@ -96,7 +96,14 @@
     def tile(dy, dx):
         return seen[dx + 1][dy % GY]
 
-    for off in range(GY):
+    gathers = []
+    if REMOTE:
+        pl.semaphore_wait(barrier, len(peers))
+        gathers = [
+            remote(c_send.at[off], c_recv.at[off], g_send.at[off], g_recv.at[off], dev(off, 0))
+            for off in range(1, GY)
+        ]
+    for off in list(range(1, GY)) + [0]:
         pick = {
             (dy, dx): tile(off + dy, dx) & 3 for dy in (-1, 0, 1) for dx in (-1, 0, 1)
         }
@@ -106,19 +113,28 @@
         corner_s = jnp.where(eastern, c_ends[pick[1, 1]], c_ends[pick[1, -1]])
         ends = jnp.where(sub < 2, c_ends[pick[-1, 0]], c_ends[pick[1, 0]])
         c_send[off, pl.ds(40, 8)] = jnp.where(sub < 4, ends, jnp.where(sub < 6, corner_n, corner_s))
-    gathers = []
-    if REMOTE:
-        pl.semaphore_wait(barrier, len(peers))
-        gathers = [
-            remote(c_send.at[off], c_recv.at[off], g_send.at[off], g_recv.at[off], dev(off, 0))
-            for off in range(1, GY)
-        ]
-        for g in gathers:
-            g.start()
+        if off > 0 and REMOTE:
+            gathers[off - 1].start()
     c_recv[0] = c_send[0]
 
     for copy in loads:
         copy.wait()
+
+    def send(at, moves):
+        copies = [
+            remote(s, d, x_send.at[at + n], x_recv.at[at + n], dev(*to)) for n, (s, d, to) in enumerate(moves)
+        ]
+        for c in copies:
+            c.start()
+        return copies
+
+    halos = []
+    first, last = pl.ds(0, HALO), pl.ds(TILE + HALO, HALO)
+    if REMOTE:
+        halos += send(0, [
+            (nat.at[:, :, pl.ds(TILE, HALO)], nat.at[:, :, first], (1, 0)),
+            (nat.at[:, :, pl.ds(HALO, HALO)], nat.at[:, :, last], (-1, 0)),
+        ])
     shifts = (0, 16, 32, 48, 56)
     for t in range(16):
         w = e = None
@@ -136,24 +152,17 @@
         pack_w[pl.ds(t * 8, 8), :] = w
         pack_e[pl.ds(t * 8, 8), :] = e
 
-    halos = []
     if REMOTE:
         half = pl.ds(HALO, 128)
         head, tail = pl.ds(0, HALO), pl.ds(112, HALO)
-        first, last = pl.ds(0, HALO), pl.ds(TILE + HALO, HALO)
-        moves = [
+        halos += send(2, [
             (pack_e, h_west.at[half], (0, 1)),
             (pack_w, h_east.at[half], (0, -1)),
-            (nat.at[:, :, pl.ds(TILE, HALO)], nat.at[:, :, first], (1, 0)),
-            (nat.at[:, :, pl.ds(HALO, HALO)], nat.at[:, :, last], (-1, 0)),
             (pack_e.at[tail], h_west.at[first], (1, 1)),
             (pack_e.at[head], h_west.at[last], (-1, 1)),
             (pack_w.at[tail], h_east.at[first], (1, -1)),
             (pack_w.at[head], h_east.at[last], (-1, -1)),
-        ]
-        halos = [remote(s, d, x_send.at[n], x_recv.at[n], dev(*to)) for n, (s, d, to) in enumerate(moves)]
-        for h in halos:
-            h.start()
+        ])
 
     inside, iced = {}, {}
     for dy, dx in near + [(0, 0)]:
@@ -236,19 +245,22 @@
             y = pltpu.roll(ref[p(0)], 96, 1)
             ref[p(GROUP)] = jnp.where(lane >= 96, pltpu.roll(y, 7, 0), y)
 
-    for h in halos:
-        h.wait()
-
-    for ref in (h_west, h_east):
-        ref[pl.ds(HALO + 128, 128)] = pltpu.roll(ref[pl.ds(HALO, 128)], 64, 1)
-        ref[pl.ds(0, HALO)] = pltpu.roll(ref[pl.ds(0, HALO)], 64, 1)
-
+    for h in halos[:2]:
+        h.wait_recv()
     fields = (T, FU, FV, OU, OV)
     for i in range(STRIP):
         at = pl.ds(i, 8, stride=STRIP)
         for c in range(2):
             for f, dst in enumerate(fields):
-                dst[m(i, c)] = nat[f, c, at, :]
+                x = nat[f, c, at, :]
+                if f == 0 and not HALO <= i < TILE + HALO - 7 * STRIP:
+                    x = jnp.where(region(i, inside) > 0.0, x, 0.0)
+                dst[m(i, c)] = x
+    for h in halos[2:]:
+        h.wait_recv()
+    for ref in (h_west, h_east):
+        ref[pl.ds(HALO + 128, 128)] = pltpu.roll(ref[pl.ds(HALO, 128)], 64, 1)
+        ref[pl.ds(0, HALO)] = pltpu.roll(ref[pl.ds(0, HALO)], 64, 1)
     for i in range(GROUP):
         right = [h_east[pl.ds(GROUP * g + i, 8, stride=STRIP), :] for g in range(4)]
         left = [h_west[pl.ds(GROUP * g + i, 8, stride=STRIP), :] for g in range(4)]
@@ -264,11 +276,6 @@
             if f == 0:
                 x = jnp.where(side_region(i, inside) > 0.0, x, 0.0)
             dst[p(i)] = x
-    for i in list(range(HALO)) + list(range(TILE + HALO - 7 * STRIP, STRIP)):
-        keep = region(i, inside) > 0.0
-        for c in range(2):
-            T[m(i, c)] = jnp.where(keep, T[m(i, c)], 0.0)
-
     base = float(visc_scale * np.power(strain_floor, -1.0 / 3.0))
     every = [[m(GROUP * g + i, c) for c in range(2) for g in range(4)] + [p(i)] for i in range(GROUP)]
 
@@ -301,13 +308,13 @@
             if spot == 1:
                 wrap([H])
 
-    def sweep(src, dst, fu_ref, fv_ref, fresh):
+    def sweep(src, dst, fu_ref, fv_ref, fresh, final=None):
         starts = list(range(0, GROUP, ROWS))
         for spot, s in enumerate([starts[0], starts[-1]] + starts[1:-1]):
             new_u = [[None] * 9 for _ in range(ROWS)]
             new_v = [[None] * 9 for _ in range(ROWS)]
             n = ROWS + 2
-            for lot in range(9):
+            for lot in range(8 if final is not None else 9):
                 spots = [step_of(every[s][lot], j - 1) for j in range(n)]
                 h = [H[at] for at in spots]
                 face = [h[j] + h[j + 1] for j in range(n - 1)]
@@ -355,6 +362,12 @@
                         fv = fv + tv + 4.0 * sv + cv
                     new_u[k][lot] = iu * fu
                     new_v[k][lot] = iv * fv
+            if final is not None:
+                for k in range(ROWS):
+                    for lot in range(8):
+                        at = every[s + k][lot]
+                        final[at] = FU[at] * new_u[k][lot] + FV[at] * new_v[k][lot]
+                continue
             for k in range(ROWS):
                 put(dst, s + k, *split(new_u[k]), *split(new_v[k]))
             if spot == 1:
@@ -426,6 +439,8 @@
             new_u.append(IU[at] * mu)
             new_v.append(IV[at] * mv)
         put(one, i, *split(new_u), *split(new_v))
+    for h in halos:
+        h.wait_send()
     for i in range(STRIP):
         at = pl.ds(i, 8, stride=STRIP)
         for c in range(2):
@@ -447,13 +462,13 @@
         sweep(one, zero, OU, OV, False)
         sweep(zero, one, OU, OV, False)
 
-    sweep(one, zero, OU, OV, False)
+    sweep(one, zero, OU, OV, False, final=T)
 
     for i in range(GROUP):
         total = None
         for k in range(4):
             j = i * 4 + k
-            cell = [FU[m(j, c)] * U0[m(j, c)] + FV[m(j, c)] * V0[m(j, c)] for c in range(2)]
+            cell = [T[m(j, c)] for c in range(2)]
             total = cell if total is None else [total[c] + cell[c] for c in range(2)]
         spots = []
         for c in range(2):
@@ -513,11 +528,11 @@
         c.start()
     gathered[gx] = total
     for c in third:
-        c.wait()
+        c.wait_recv()
     for g in range(GX):
         for j in range(4):
             out_g[:, pl.ds((4 * g + j) * 128, 128)] = gathered[g, pl.ds(4 * j, 4)]
-    for c in gathers + first + second:
+    for c in gathers + first + second + third:
         c.wait_send()
     for s in stores:
         s.wait()

time: 48.7 us -> 48.5 us (level)
  no operation moved by 1% of the time
where the time goes in v6:
time: 48.5 us; the launch traced here: 48.3 us
  Pallas kernels  44.4 us (92%)
  local copies, waits for them, and re-layouts  3.21 us (7%)
  between operations  0.65 us (1%)
    pallas_call x1, Pallas kernels, call(): pl.pallas_call(kernel, name='friction_gradient', out_shape=(shape((TILE,...  44.4 us
    unnamed x7, local copies, waits for them, and re-layouts  3.21 us

profile of v6, /device:TPU:0, one launch (start us, length us, event | category | flops | bytes accessed | tf_op | source)
XLA Modules:
  0.0 48.3 jit_solution(8266585571394824873)
XLA Ops:
  0.6 44.4 %friction_gradient.1 = (f32[256,256]{1,0:T(8,128)}, f32[256,256]{1,0:T(8,128)}, f32[4,4096]{1,0:T(4,128)}) custom-call(s32[8,1,16]{2,1,0:T(1,128)} %bitcast.2, s32[8,16]{1,0:T(8,128)} %bitcast.3, f32[256,256]{1,0:T(8,128)} %thick.1, f32[2,256,256]{2,1,0:T(8,128)} %drv.1, f32[2,256,256]{2,1,0:T(8,128)} %obs.1, f32[4,4096]{1,0:T(4,128)} %ctl.1), custom_call_target="tpu_custom_call" | custom-call | tf_op jit(solution)/shard_map/friction_gradient/pallas_call | solution.py:549
  45.0 0.0 copy-start
  45.0 1.7 %copy.12 = f32[256,256]{1,0:T(8,128)} copy(f32[256,256]{1,0:T(8,128)} %get-tuple-element.6) | data formatting | bytes 524288
  46.8 0.0 copy-done
  46.8 0.0 copy-start.1
  46.8 0.7 %copy.13 = f32[256,256]{1,0:T(8,128)} copy(f32[256,256]{1,0:T(8,128)S(1)} %copy-done) | data formatting | bytes 524288
  47.5 0.2 copy-done.1
  47.6 0.6 %copy.14 = f32[4,4096]{1,0:T(4,128)} copy(f32[4,4096]{1,0:T(4,128)S(1)} %copy-done.1) | data formatting | bytes 131072
Async XLA Ops:
  45.0 1.7 %copy-start = (f32[256,256]{1,0:T(8,128)S(1)}, f32[256,256]{1,0:T(8,128)}, u32[]{:S(2)}) copy-start(f32[256,256]{1,0:T(8,128)} %get-tuple-element.7) | copy-start | bytes 786436
  46.8 0.9 %copy-start.1 = (f32[4,4096]{1,0:T(4,128)S(1)}, f32[4,4096]{1,0:T(4,128)}, u32[]{:S(2)}) copy-start(f32[4,4096]{1,0:T(4,128)} %get-tuple-element.8) | copy-start | bytes 196612

commit v7 on v6

--- a/solution.py
+++ b/solution.py
@@ -16,6 +16,7 @@
 GX = 8
 GY = 16
 ROWS = 3
+PARTS = 2
 REMOTE = True
 MESH = pl.DeviceIdType.MESH
 F32 = jnp.float32
@@ -590,10 +591,48 @@
     )(*operands)
 
 
+def copy_kernel(u, v, g, out_u, out_v, out_g, via, via_g, sem_in, sem_out):
+    part = TILE // PARTS
+    moves = []
+    for n, (src, dst) in enumerate(((u, out_u), (v, out_v))):
+        for k in range(PARTS):
+            rows = pl.ds(k * part, part)
+            moves.append((src.at[rows], via.at[n, rows], dst.at[rows]))
+    moves.append((g, via_g, out_g))
+    into = [pltpu.make_async_copy(a, b, sem_in.at[n]) for n, (a, b, _) in enumerate(moves)]
+    out = [pltpu.make_async_copy(b, c, sem_out.at[n]) for n, (_, b, c) in enumerate(moves)]
+    for c in into:
+        c.start()
+    for a, b in zip(into, out):
+        a.wait()
+        b.start()
+    for c in out:
+        c.wait()
+
+
+def hand_out(*arrays):
+    hbm = pl.BlockSpec(memory_space=pltpu.HBM)
+    return pl.pallas_call(
+        copy_kernel,
+        name="hand_out",
+        out_shape=tuple(jax.ShapeDtypeStruct(a.shape, F32) for a in arrays),
+        in_specs=[hbm] * 3,
+        out_specs=[hbm] * 3,
+        scratch_shapes=[
+            pltpu.VMEM((2, TILE, TILE), F32),
+            pltpu.VMEM((4, 4096), F32),
+            pltpu.SemaphoreType.DMA((2 * PARTS + 1,)),
+            pltpu.SemaphoreType.DMA((2 * PARTS + 1,)),
+        ],
+        compiler_params=pltpu.CompilerParams(vmem_limit_bytes=60 << 20),
+    )(*arrays)
+
+
 def per_device(thickness, driving, observed, control, ice_mask, tile_block):
-    return call(
+    results = call(
         tile_block.transpose(1, 2, 0), ice_mask.T, thickness, driving, observed, control
     )
+    return hand_out(*results)
 
 
 def solution(mesh):

time: 48.5 us -> 47.1 us (0.971)
  local copies, waits for them, and re-layouts: 3.21 us -> 0 us
  Pallas kernels: 44.4 us -> 46.3 us
    unnamed x7 -> x0, local copies, waits for them, and re-layouts: 3.21 us -> none
    pallas_call x0 -> x1, Pallas kernels: none -> 1.85 us  [hand_out(): pl.pallas_call(copy_kernel, name='hand_out', out_shape=tuple((jax.ShapeDt...]
where the time goes in v7:
time: 47.1 us; the launch traced here: 46.9 us
  Pallas kernels  46.3 us (98%)
  between operations  0.64 us (1%)
    pallas_call x1, Pallas kernels, call(): pl.pallas_call(kernel, name='friction_gradient', out_shape=(shape((TILE,...  44.4 us
    pallas_call x1, Pallas kernels, hand_out(): pl.pallas_call(copy_kernel, name='hand_out', out_shape=tuple((jax.ShapeDt...  1.85 us

profile of v7, /device:TPU:0, one launch (start us, length us, event | category | flops | bytes accessed | tf_op | source)
XLA Modules:
  0.0 46.9 jit_solution(16869000752041776515)
XLA Ops:
  0.6 44.4 %friction_gradient.1 = (f32[256,256]{1,0:T(8,128)}, f32[256,256]{1,0:T(8,128)}, f32[4,4096]{1,0:T(4,128)}) custom-call(s32[8,1,16]{2,1,0:T(1,128)} %bitcast.2, s32[8,16]{1,0:T(8,128)} %bitcast.3, f32[256,256]{1,0:T(8,128)} %thick.1, f32[2,256,256]{2,1,0:T(8,128)} %drv.1, f32[2,256,256]{2,1,0:T(8,128)} %obs.1, f32[4,4096]{1,0:T(4,128)} %ctl.1), custom_call_target="tpu_custom_call" | custom-call | tf_op jit(solution)/shard_map/friction_gradient/pallas_call | solution.py:550
  45.0 1.9 %hand_out.1 = (f32[256,256]{1,0:T(8,128)}, f32[256,256]{1,0:T(8,128)}, f32[4,4096]{1,0:T(4,128)}) custom-call(f32[256,256]{1,0:T(8,128)} %get-tuple-element.6.u, f32[256,256]{1,0:T(8,128)} %get-tuple-element.7.v, f32[4,4096]{1,0:T(4,128)} %get-tuple-element.8.g), custom_call_target="tpu_custom_call" | custom-call | tf_op jit(solution)/shard_map/hand_out/pallas_call | solution.py:615
